TPU v7x, 768 devices: a whole 4x8x12 slice. The times are simulated.
768 devices in a mesh: tile: 12 (over z_hi, x), lev: 64 (over z_lo, y, core).
Axes of the slice: x: 4, y: 8, z: 12 (z_hi: 3, z_lo: 4; z = z_hi * 4 + z_lo), core: 2. Of those that a mesh axis runs over, the one named last changes fastest.
Arguments:
- control: float32 [64, 768, 1024], P('lev', 'tile'), may hold values from -6 to 6
- gain: float32 [64, 768, 1024], P('lev', 'tile'), may hold values from 0.25 to 1.75
- north_coef: float32 [64, 768, 1024], P('lev', 'tile'), may hold values from 0.02 to 0.24
- east_coef: float32 [64, 768, 1024], P('lev', 'tile'), may hold values from 0.02 to 0.24
- land_sea: int32 [64, 768, 1024], P('lev', 'tile'), may hold values 0 or 1
- region: int32 [768, 1024], P(('tile', 'lev')), may hold values from 0 to 15
- tiles: float32 [16, 2, 32, 32], replicated, may hold values from -0.5 to 1.5
Outputs:
- increment: float32 [64, 768, 1024], P('lev', 'tile')
All inputs are finite; a program needn't handle non-finite values. No bound on the sum of `land_sea` on one device may be relied on, other than what follows from the above.
Results may differ from a plain program's by a relative error of at most 0.0003.
Values sent between devices are 32-bit elements; how exact they have to be, the bound alone decides.
A program may use at most 32 MiB of HBM per device.

v0:
```python
import jax
import jax.numpy as jnp
from jax import lax
from jax.sharding import PartitionSpec as P

FIELDS = 2
LEVELS = 32
STEPS = 10
REGIONS = 16


def padded(cells, sides, width):
    for axis, dim in sides:
        count = lax.axis_size(axis)
        ends = count - 1
        head = lax.slice_in_dim(cells, 0, width, axis=dim)
        tail = lax.slice_in_dim(cells, cells.shape[dim] - width, cells.shape[dim], axis=dim)
        cells = jnp.concatenate(
            [
                lax.ppermute(tail, axis, [(i, (i + 1) % count) for i in range(ends)]),
                cells,
                lax.ppermute(head, axis, [((i + 1) % count, i) for i in range(ends)]),
            ],
            axis=dim,
        )
    return cells


def shifted(block, axis, distance):
    devices = range(lax.axis_size(axis))
    route = [(i - distance, i) for i in devices if i - distance in devices]
    return lax.ppermute(block, axis, route)


def diffusion_step(field, north_face, east_face, ocean):
    centre = field[:, 1:-1]
    north = north_face[:, 1:-1] * (field[:, 2:] - centre)
    south = north_face[:, :-2] * (centre - field[:, :-2])
    border = jnp.zeros_like(centre[:, :, :1])
    eastward = jnp.concatenate([centre[:, :, 1:], border], axis=2)
    east_flux = east_face[:, 1:-1] * (eastward - centre)
    west_flux = jnp.concatenate([border, east_flux[:, :, :-1]], axis=2)
    return ocean[:, 1:-1] * (centre + north - south + east_flux - west_flux)


def diffuse(field, north_face, east_face, ocean):
    for repeat in range(STEPS):
        extended = padded(field, (("tile", 1),), 1)
        field = diffusion_step(extended, north_face, east_face, ocean)
    return field


def regional_apply(matrices, column, selected):
    products = jnp.einsum("rfij,fjc->rfic", matrices, column, precision=lax.Precision.HIGHEST)
    return jnp.sum(jnp.where(selected[:, None, None, :], products, jnp.float32(0.0)), axis=0)


def pad_rows(array):
    return jnp.pad(array, ((0, 0), (1, 1), (0, 0)))


def body(control, gain, north_coef, east_coef, land_sea, region, tiles):
    ocean = land_sea.astype(jnp.float32)
    below_row = shifted(north_coef[:, -1:], "tile", 1)
    upper_zero = jnp.zeros_like(below_row)
    north_face = jnp.concatenate([below_row, north_coef, upper_zero], axis=1)
    east_face = pad_rows(east_coef)
    ocean_rim = pad_rows(ocean)
    forward = diffuse(ocean * gain * control, north_face, east_face, ocean_rim)
    slab_count, row_count, col_count = forward.shape
    column = lax.all_to_all(
        forward.reshape(slab_count, row_count * col_count),
        "lev",
        split_axis=1,
        concat_axis=0,
        tiled=True,
    )
    cell_count = column.shape[1]
    column = column.reshape(FIELDS, LEVELS, cell_count)
    selected = region.reshape(-1)[None, :] == jnp.arange(REGIONS, dtype=jnp.int32)[:, None]
    column_out = regional_apply(tiles, column, selected)
    mixed = regional_apply(jnp.swapaxes(tiles, 2, 3), column_out, selected)
    returned = lax.all_to_all(
        mixed.reshape(FIELDS * LEVELS, cell_count), "lev", split_axis=0, concat_axis=1, tiled=True
    )
    field = ocean * returned.reshape(slab_count, row_count, col_count)
    return gain * diffuse(field, north_face, east_face, ocean_rim)


def solution(mesh):
    return jax.shard_map(
        body,
        mesh=mesh,
        in_specs=(
            P("lev", "tile", None),
            P("lev", "tile", None),
            P("lev", "tile", None),
            P("lev", "tile", None),
            P("lev", "tile", None),
            P(("tile", "lev"), None),
            P(),
        ),
        out_specs=P("lev", "tile", None),
        check_vma=False,
    )
```

profile of v0, /device:TPU:6, one launch (start us, length us, event | category | flops | bytes accessed | tf_op | source)
XLA Modules:
  0.0 348.9 jit_solution(7247202845327002895)
XLA Ops:
  0.8 10.8 %collective-permute-start.1 = (f32[1,1,1024]{2,1,0:T(1,128)S(1)}, f32[1,1,1024]{2,1,0:T(1,128)S(1)}, u32[]{:S(2)}, u32[]{:S(2)}) collective-permute-start(f32[1,1,1024]{2,1,0:T(1,128)S(1)} %slice.468), channel_id=1, source_target_pairs={{0,64},{64,128},{128,192},{192,256},{256,320},{320,384},{384,448},... | collective-permute-start | bytes 12296 | tf_op jit(solution)/shard_map/ppermute | solution.py:32
  12.8 2.1 collective-permute-start
  14.9 9.9 %collective-permute-start.2 = (f32[1,1,1024]{2,1,0:T(1,128)S(1)}, f32[1,1,1024]{2,1,0:T(1,128)S(1)}, u32[]{:S(2)}, u32[]{:S(2)}) collective-permute-start(f32[1,1,1024]{2,1,0:T(1,128)S(1)} %get-tuple-element.44), channel_id=1, source_target_pairs={{0,64},{64,128},{128,192},{192,256},{256,320},{320,384},{384,448},... | collective-permute-start | bytes 12296 | tf_op jit(solution)/shard_map/ppermute | solution.py:20
  26.5 1.9 collective-permute-start.3
  28.4 10.2 %collective-permute-start.4 = (f32[1,1,1024]{2,1,0:T(1,128)S(1)}, f32[1,1,1024]{2,1,0:T(1,128)S(1)}, u32[]{:S(2)}, u32[]{:S(2)}) collective-permute-start(f32[1,1,1024]{2,1,0:T(1,128)S(1)} %get-tuple-element.42), channel_id=1, source_target_pairs={{0,64},{64,128},{128,192},{192,256},{256,320},{320,384},{384,448},... | collective-permute-start | bytes 12296 | tf_op jit(solution)/shard_map/ppermute | solution.py:20
  38.7 1.2 collective-permute-done.4
  40.2 1.9 collective-permute-start.5
  42.2 10.2 %collective-permute-start.6 = (f32[1,1,1024]{2,1,0:T(1,128)S(1)}, f32[1,1,1024]{2,1,0:T(1,128)S(1)}, u32[]{:S(2)}, u32[]{:S(2)}) collective-permute-start(f32[1,1,1024]{2,1,0:T(1,128)S(1)} %get-tuple-element.40), channel_id=1, source_target_pairs={{0,64},{64,128},{128,192},{192,256},{256,320},{320,384},{384,448},... | collective-permute-start | bytes 12296 | tf_op jit(solution)/shard_map/ppermute | solution.py:20
  54.0 1.9 collective-permute-start.7
  55.9 10.2 %collective-permute-start.8 = (f32[1,1,1024]{2,1,0:T(1,128)S(1)}, f32[1,1,1024]{2,1,0:T(1,128)S(1)}, u32[]{:S(2)}, u32[]{:S(2)}) collective-permute-start(f32[1,1,1024]{2,1,0:T(1,128)S(1)} %get-tuple-element.38), channel_id=1, source_target_pairs={{0,64},{64,128},{128,192},{192,256},{256,320},{320,384},{384,448},... | collective-permute-start | bytes 12296 | tf_op jit(solution)/shard_map/ppermute | solution.py:20
  67.8 10.2 %collective-permute-start.10 = (f32[1,1,1024]{2,1,0:T(1,128)S(1)}, f32[1,1,1024]{2,1,0:T(1,128)S(1)}, u32[]{:S(2)}, u32[]{:S(2)}) collective-permute-start(f32[1,1,1024]{2,1,0:T(1,128)S(1)} %get-tuple-element.36), channel_id=1, source_target_pairs={{0,64},{64,128},{128,192},{192,256},{256,320},{320,384},{384,448},... | collective-permute-start | bytes 12296 | tf_op jit(solution)/shard_map/ppermute | solution.py:20
  78.0 1.9 collective-permute-start.9
  80.0 9.5 %collective-permute-done.9 = f32[1,1,1024]{2,1,0:T(1,128)S(1)} collective-permute-done((f32[1,1,1024]{2,1,0:T(1,128)S(1)}, f32[1,1,1024]{2,1,0:T(1,128)S(1)}, u32[]{:S(2)}, u32[]{:S(2)}) %collective-permute-start.9) | collective-permute-done | bytes 4128 | tf_op jit(solution)/shard_map/ppermute | solution.py:22
  89.8 1.9 collective-permute-start.11
  91.8 9.9 %collective-permute-start.12 = (f32[1,1,1024]{2,1,0:T(1,128)S(1)}, f32[1,1,1024]{2,1,0:T(1,128)S(1)}, u32[]{:S(2)}, u32[]{:S(2)}) collective-permute-start(f32[1,1,1024]{2,1,0:T(1,128)S(1)} %get-tuple-element.34), channel_id=1, source_target_pairs={{0,64},{64,128},{128,192},{192,256},{256,320},{320,384},{384,448},... | collective-permute-start | bytes 12296 | tf_op jit(solution)/shard_map/ppermute | solution.py:20
  103.3 1.9 collective-permute-start.13
  105.3 10.2 %collective-permute-start.14 = (f32[1,1,1024]{2,1,0:T(1,128)S(1)}, f32[1,1,1024]{2,1,0:T(1,128)S(1)}, u32[]{:S(2)}, u32[]{:S(2)}) collective-permute-start(f32[1,1,1024]{2,1,0:T(1,128)S(1)} %get-tuple-element.32), channel_id=1, source_target_pairs={{0,64},{64,128},{128,192},{192,256},{256,320},{320,384},{384,448},... | collective-permute-start | bytes 12296 | tf_op jit(solution)/shard_map/ppermute | solution.py:20
  117.1 1.9 collective-permute-start.15
  119.0 10.2 %collective-permute-start.16 = (f32[1,1,1024]{2,1,0:T(1,128)S(1)}, f32[1,1,1024]{2,1,0:T(1,128)S(1)}, u32[]{:S(2)}, u32[]{:S(2)}) collective-permute-start(f32[1,1,1024]{2,1,0:T(1,128)S(1)} %get-tuple-element.30), channel_id=1, source_target_pairs={{0,64},{64,128},{128,192},{192,256},{256,320},{320,384},{384,448},... | collective-permute-start | bytes 12296 | tf_op jit(solution)/shard_map/ppermute | solution.py:20
  130.9 1.9 collective-permute-start.17
  132.8 10.2 %collective-permute-start.18 = (f32[1,1,1024]{2,1,0:T(1,128)S(1)}, f32[1,1,1024]{2,1,0:T(1,128)S(1)}, u32[]{:S(2)}, u32[]{:S(2)}) collective-permute-start(f32[1,1,1024]{2,1,0:T(1,128)S(1)} %get-tuple-element.28), channel_id=1, source_target_pairs={{0,64},{64,128},{128,192},{192,256},{256,320},{320,384},{384,448},... | collective-permute-start | bytes 12296 | tf_op jit(solution)/shard_map/ppermute | solution.py:20
  144.6 1.9 collective-permute-start.19
  146.6 10.2 %collective-permute-start.20 = (f32[1,1,1024]{2,1,0:T(1,128)S(1)}, f32[1,1,1024]{2,1,0:T(1,128)S(1)}, u32[]{:S(2)}, u32[]{:S(2)}) collective-permute-start(f32[1,1,1024]{2,1,0:T(1,128)S(1)} %get-tuple-element.26), channel_id=1, source_target_pairs={{0,64},{64,128},{128,192},{192,256},{256,320},{320,384},{384,448},... | collective-permute-start | bytes 12296 | tf_op jit(solution)/shard_map/ppermute | solution.py:20
  159.2 13.2 %all-to-all-start = ((f32[1,64,1024]{2,0,1:T(1,128)}), f32[1,64,1024]{2,0,1:T(1,128)S(1)}, u32[]{:S(2)}, u32[]{:S(2)}) async-start(f32[1,64,1024]{2,0,1:T(1,128)} %copy.274), calls=%async_computation | async-start | bytes 524288 | tf_op jit(solution)/shard_map/all_to_all | solution.py:71
  172.5 12.4 %all-to-all-done = f32[1,64,1024]{2,0,1:T(1,128)S(1)} async-done(((f32[1,64,1024]{2,0,1:T(1,128)}), f32[1,64,1024]{2,0,1:T(1,128)S(1)}, u32[]{:S(2)}, u32[]{:S(2)}) %all-to-all-start) | async-done | bytes 262176 | tf_op jit(solution)/shard_map/all_to_all | solution.py:71
  185.0 3.7 %fusion.1 = f32[2,32,1024]{2,1,0:T(8,128)S(1)} fusion(f32[2,32,1024,1]{2,1,3,0:T(8,128)S(1)} %bitcast.64, pred[16,1024]{1,0:T(8,128)(4,1)S(1)} %iota_compare_fusion, f32[16,2,32,32]{3,2,1,0:T(8,128)S(1)} %copy-done), kind=kOutput, calls=%fused_computation.3 | convolution fusion | flops 404684800 | bytes 671744 | tf_op jit(solution)/shard_map/rfij,fjc->rfic/dot_general | solution.py:54
  188.7 3.8 %fusion = f32[2,32,1024]{2,1,0:T(8,128)S(1)} fusion(pred[16,1024]{1,0:T(8,128)(4,1)S(1)} %iota_compare_fusion, f32[2,32,1024]{2,1,0:T(8,128)S(1)} %fusion.1, f32[16,2,32,32]{3,2,1,0:T(8,128)S(1)} %copy-done), kind=kOutput, calls=%fused_computation.1 | convolution fusion | flops 404684800 | bytes 671744 | tf_op jit(solution)/shard_map/rfij,fjc->rfic/dot_general | solution.py:54
  192.9 17.4 %all_to_all.23 = f32[64,1,1024]{2,1,0:T(1,128)S(1)} all-to-all(f32[64,1,1024]{2,1,0:T(1,128)S(1)} %all_to_all.9), channel_id=1, replica_groups=mesh['tile'=12,'lev'=64] {'lev'}, dimensions={0} | all-to-all | bytes 524288 | tf_op jit(solution)/shard_map/all_to_all | solution.py:83
  210.5 1.9 collective-permute-start.21
  212.5 10.2 %collective-permute-start.22 = (f32[1,1,1024]{2,1,0:T(1,128)S(1)}, f32[1,1,1024]{2,1,0:T(1,128)S(1)}, u32[]{:S(2)}, u32[]{:S(2)}) collective-permute-start(f32[1,1,1024]{2,1,0:T(1,128)S(1)} %get-tuple-element.24), channel_id=1, source_target_pairs={{0,64},{64,128},{128,192},{192,256},{256,320},{320,384},{384,448},... | collective-permute-start | bytes 12296 | tf_op jit(solution)/shard_map/ppermute | solution.py:20
  224.3 1.9 collective-permute-start.23
  226.2 10.2 %collective-permute-start.24 = (f32[1,1,1024]{2,1,0:T(1,128)S(1)}, f32[1,1,1024]{2,1,0:T(1,128)S(1)}, u32[]{:S(2)}, u32[]{:S(2)}) collective-permute-start(f32[1,1,1024]{2,1,0:T(1,128)S(1)} %get-tuple-element.22), channel_id=1, source_target_pairs={{0,64},{64,128},{128,192},{192,256},{256,320},{320,384},{384,448},... | collective-permute-start | bytes 12296 | tf_op jit(solution)/shard_map/ppermute | solution.py:20
  238.1 1.9 collective-permute-start.25
  240.0 10.4 %collective-permute-start.26 = (f32[1,1,1024]{2,1,0:T(1,128)S(1)}, f32[1,1,1024]{2,1,0:T(1,128)S(1)}, u32[]{:S(2)}, u32[]{:S(2)}) collective-permute-start(f32[1,1,1024]{2,1,0:T(1,128)S(1)} %get-tuple-element.20), channel_id=1, source_target_pairs={{0,64},{64,128},{128,192},{192,256},{256,320},{320,384},{384,448},... | collective-permute-start | bytes 12296 | tf_op jit(solution)/shard_map/ppermute | solution.py:20
  251.8 1.9 collective-permute-start.27
  253.8 10.2 %collective-permute-start.28 = (f32[1,1,1024]{2,1,0:T(1,128)S(1)}, f32[1,1,1024]{2,1,0:T(1,128)S(1)}, u32[]{:S(2)}, u32[]{:S(2)}) collective-permute-start(f32[1,1,1024]{2,1,0:T(1,128)S(1)} %get-tuple-element.18), channel_id=1, source_target_pairs={{0,64},{64,128},{128,192},{192,256},{256,320},{320,384},{384,448},... | collective-permute-start | bytes 12296 | tf_op jit(solution)/shard_map/ppermute | solution.py:20
  265.6 1.9 collective-permute-start.29
  267.5 10.2 %collective-permute-start.30 = (f32[1,1,1024]{2,1,0:T(1,128)S(1)}, f32[1,1,1024]{2,1,0:T(1,128)S(1)}, u32[]{:S(2)}, u32[]{:S(2)}) collective-permute-start(f32[1,1,1024]{2,1,0:T(1,128)S(1)} %get-tuple-element.16), channel_id=1, source_target_pairs={{0,64},{64,128},{128,192},{192,256},{256,320},{320,384},{384,448},... | collective-permute-start | bytes 12296 | tf_op jit(solution)/shard_map/ppermute | solution.py:20
  279.4 1.9 collective-permute-start.31
  281.3 10.2 %collective-permute-start.32 = (f32[1,1,1024]{2,1,0:T(1,128)S(1)}, f32[1,1,1024]{2,1,0:T(1,128)S(1)}, u32[]{:S(2)}, u32[]{:S(2)}) collective-permute-start(f32[1,1,1024]{2,1,0:T(1,128)S(1)} %get-tuple-element.14), channel_id=1, source_target_pairs={{0,64},{64,128},{128,192},{192,256},{256,320},{320,384},{384,448},... | collective-permute-start | bytes 12296 | tf_op jit(solution)/shard_map/ppermute | solution.py:20
  293.1 1.9 collective-permute-start.33
  295.1 10.2 %collective-permute-start.34 = (f32[1,1,1024]{2,1,0:T(1,128)S(1)}, f32[1,1,1024]{2,1,0:T(1,128)S(1)}, u32[]{:S(2)}, u32[]{:S(2)}) collective-permute-start(f32[1,1,1024]{2,1,0:T(1,128)S(1)} %get-tuple-element.12), channel_id=1, source_target_pairs={{0,64},{64,128},{128,192},{192,256},{256,320},{320,384},{384,448},... | collective-permute-start | bytes 12296 | tf_op jit(solution)/shard_map/ppermute | solution.py:20
  306.9 1.9 collective-permute-start.35
  308.8 10.2 %collective-permute-start.36 = (f32[1,1,1024]{2,1,0:T(1,128)S(1)}, f32[1,1,1024]{2,1,0:T(1,128)S(1)}, u32[]{:S(2)}, u32[]{:S(2)}) collective-permute-start(f32[1,1,1024]{2,1,0:T(1,128)S(1)} %get-tuple-element.10), channel_id=1, source_target_pairs={{0,64},{64,128},{128,192},{192,256},{256,320},{320,384},{384,448},... | collective-permute-start | bytes 12296 | tf_op jit(solution)/shard_map/ppermute | solution.py:20
  320.7 1.9 collective-permute-start.37
  322.6 10.2 %collective-permute-start.38 = (f32[1,1,1024]{2,1,0:T(1,128)S(1)}, f32[1,1,1024]{2,1,0:T(1,128)S(1)}, u32[]{:S(2)}, u32[]{:S(2)}) collective-permute-start(f32[1,1,1024]{2,1,0:T(1,128)S(1)} %get-tuple-element.8), channel_id=1, source_target_pairs={{0,64},{64,128},{128,192},{192,256},{256,320},{320,384},{384,448},... | collective-permute-start | bytes 12296 | tf_op jit(solution)/shard_map/ppermute | solution.py:20
  334.4 1.9 collective-permute-start.39
  336.4 10.3 %collective-permute-start.40 = (f32[1,1,1024]{2,1,0:T(1,128)S(1)}, f32[1,1,1024]{2,1,0:T(1,128)S(1)}, u32[]{:S(2)}, u32[]{:S(2)}) collective-permute-start(f32[1,1,1024]{2,1,0:T(1,128)S(1)} %get-tuple-element.6), channel_id=1, source_target_pairs={{0,64},{64,128},{128,192},{192,256},{256,320},{320,384},{384,448},... | collective-permute-start | bytes 12296 | tf_op jit(solution)/shard_map/ppermute | solution.py:20
  (138 shorter events, 33.2 us)
Async XLA Ops:
  0.0 185.0 %copy-start = (f32[16,2,32,32]{3,2,1,0:T(8,128)S(1)}, f32[16,2,32,32]{3,2,1,0:T(8,128)}, u32[]{:S(2)}) copy-start(f32[16,2,32,32]{3,2,1,0:T(8,128)} %param.13) | copy-start | bytes 393220
  0.8 24.2 %collective-permute-start.1 = (f32[1,1,1024]{2,1,0:T(1,128)S(1)}, f32[1,1,1024]{2,1,0:T(1,128)S(1)}, u32[]{:S(2)}, u32[]{:S(2)}) collective-permute-start(f32[1,1,1024]{2,1,0:T(1,128)S(1)} %slice.468), channel_id=1, source_target_pairs={{0,64},{64,128},{128,192},{192,256},{256,320},{320,384},{384,448},... | collective-permute-start | bytes 12296 | tf_op jit(solution)/shard_map/ppermute | solution.py:32
  12.8 12.2 %copy-start.3 = (f32[1,64,1024]{2,1,0:T(8,128)S(1)}, f32[1,64,1024]{2,1,0:T(8,128)}, u32[]{:S(2)}) copy-start(f32[1,64,1024]{2,1,0:T(8,128)} %param.10) | copy-start | bytes 786436
  12.8 12.2 %collective-permute-start = (f32[1,1,1024]{2,1,0:T(1,128)S(1)}, f32[1,1,1024]{2,1,0:T(1,128)S(1)}, u32[]{:S(2)}, u32[]{:S(2)}) collective-permute-start(f32[1,1,1024]{2,1,0:T(1,128)S(1)} %get-tuple-element.43), channel_id=1, source_target_pairs={{64,0},{128,64},{192,128},{256,192},{320,256},{384,320},{448,384},... | collective-permute-start | bytes 12296 | tf_op jit(solution)/shard_map/ppermute | solution.py:22
  14.9 11.3 %collective-permute-start.2 = (f32[1,1,1024]{2,1,0:T(1,128)S(1)}, f32[1,1,1024]{2,1,0:T(1,128)S(1)}, u32[]{:S(2)}, u32[]{:S(2)}) collective-permute-start(f32[1,1,1024]{2,1,0:T(1,128)S(1)} %get-tuple-element.44), channel_id=1, source_target_pairs={{0,64},{64,128},{128,192},{192,256},{256,320},{320,384},{384,448},... | collective-permute-start | bytes 12296 | tf_op jit(solution)/shard_map/ppermute | solution.py:20
  25.0 1.2 copy-start.1
  25.0 1.2 copy-start.2
  26.5 12.2 %collective-permute-start.3 = (f32[1,1,1024]{2,1,0:T(1,128)S(1)}, f32[1,1,1024]{2,1,0:T(1,128)S(1)}, u32[]{:S(2)}, u32[]{:S(2)}) collective-permute-start(f32[1,1,1024]{2,1,0:T(1,128)S(1)} %get-tuple-element.41), channel_id=1, source_target_pairs={{64,0},{128,64},{192,128},{256,192},{320,256},{384,320},{448,384},... | collective-permute-start | bytes 12296 | tf_op jit(solution)/shard_map/ppermute | solution.py:22
  28.4 11.5 %collective-permute-start.4 = (f32[1,1,1024]{2,1,0:T(1,128)S(1)}, f32[1,1,1024]{2,1,0:T(1,128)S(1)}, u32[]{:S(2)}, u32[]{:S(2)}) collective-permute-start(f32[1,1,1024]{2,1,0:T(1,128)S(1)} %get-tuple-element.42), channel_id=1, source_target_pairs={{0,64},{64,128},{128,192},{192,256},{256,320},{320,384},{384,448},... | collective-permute-start | bytes 12296 | tf_op jit(solution)/shard_map/ppermute | solution.py:20
  40.2 12.2 %collective-permute-start.5 = (f32[1,1,1024]{2,1,0:T(1,128)S(1)}, f32[1,1,1024]{2,1,0:T(1,128)S(1)}, u32[]{:S(2)}, u32[]{:S(2)}) collective-permute-start(f32[1,1,1024]{2,1,0:T(1,128)S(1)} %get-tuple-element.39), channel_id=1, source_target_pairs={{64,0},{128,64},{192,128},{256,192},{320,256},{384,320},{448,384},... | collective-permute-start | bytes 12296 | tf_op jit(solution)/shard_map/ppermute | solution.py:22
  42.2 11.5 %collective-permute-start.6 = (f32[1,1,1024]{2,1,0:T(1,128)S(1)}, f32[1,1,1024]{2,1,0:T(1,128)S(1)}, u32[]{:S(2)}, u32[]{:S(2)}) collective-permute-start(f32[1,1,1024]{2,1,0:T(1,128)S(1)} %get-tuple-element.40), channel_id=1, source_target_pairs={{0,64},{64,128},{128,192},{192,256},{256,320},{320,384},{384,448},... | collective-permute-start | bytes 12296 | tf_op jit(solution)/shard_map/ppermute | solution.py:20
  54.0 12.2 %collective-permute-start.7 = (f32[1,1,1024]{2,1,0:T(1,128)S(1)}, f32[1,1,1024]{2,1,0:T(1,128)S(1)}, u32[]{:S(2)}, u32[]{:S(2)}) collective-permute-start(f32[1,1,1024]{2,1,0:T(1,128)S(1)} %get-tuple-element.37), channel_id=1, source_target_pairs={{64,0},{128,64},{192,128},{256,192},{320,256},{384,320},{448,384},... | collective-permute-start | bytes 12296 | tf_op jit(solution)/shard_map/ppermute | solution.py:22
  55.9 11.5 %collective-permute-start.8 = (f32[1,1,1024]{2,1,0:T(1,128)S(1)}, f32[1,1,1024]{2,1,0:T(1,128)S(1)}, u32[]{:S(2)}, u32[]{:S(2)}) collective-permute-start(f32[1,1,1024]{2,1,0:T(1,128)S(1)} %get-tuple-element.38), channel_id=1, source_target_pairs={{0,64},{64,128},{128,192},{192,256},{256,320},{320,384},{384,448},... | collective-permute-start | bytes 12296 | tf_op jit(solution)/shard_map/ppermute | solution.py:20
  67.8 12.2 %collective-permute-start.10 = (f32[1,1,1024]{2,1,0:T(1,128)S(1)}, f32[1,1,1024]{2,1,0:T(1,128)S(1)}, u32[]{:S(2)}, u32[]{:S(2)}) collective-permute-start(f32[1,1,1024]{2,1,0:T(1,128)S(1)} %get-tuple-element.36), channel_id=1, source_target_pairs={{0,64},{64,128},{128,192},{192,256},{256,320},{320,384},{384,448},... | collective-permute-start | bytes 12296 | tf_op jit(solution)/shard_map/ppermute | solution.py:20
  78.0 11.5 %collective-permute-start.9 = (f32[1,1,1024]{2,1,0:T(1,128)S(1)}, f32[1,1,1024]{2,1,0:T(1,128)S(1)}, u32[]{:S(2)}, u32[]{:S(2)}) collective-permute-start(f32[1,1,1024]{2,1,0:T(1,128)S(1)} %get-tuple-element.35), channel_id=1, source_target_pairs={{64,0},{128,64},{192,128},{256,192},{320,256},{384,320},{448,384},... | collective-permute-start | bytes 12296 | tf_op jit(solution)/shard_map/ppermute | solution.py:22
  89.8 11.9 %collective-permute-start.11 = (f32[1,1,1024]{2,1,0:T(1,128)S(1)}, f32[1,1,1024]{2,1,0:T(1,128)S(1)}, u32[]{:S(2)}, u32[]{:S(2)}) collective-permute-start(f32[1,1,1024]{2,1,0:T(1,128)S(1)} %get-tuple-element.33), channel_id=1, source_target_pairs={{64,0},{128,64},{192,128},{256,192},{320,256},{384,320},{448,384},... | collective-permute-start | bytes 12296 | tf_op jit(solution)/shard_map/ppermute | solution.py:22
  91.8 11.3 %collective-permute-start.12 = (f32[1,1,1024]{2,1,0:T(1,128)S(1)}, f32[1,1,1024]{2,1,0:T(1,128)S(1)}, u32[]{:S(2)}, u32[]{:S(2)}) collective-permute-start(f32[1,1,1024]{2,1,0:T(1,128)S(1)} %get-tuple-element.34), channel_id=1, source_target_pairs={{0,64},{64,128},{128,192},{192,256},{256,320},{320,384},{384,448},... | collective-permute-start | bytes 12296 | tf_op jit(solution)/shard_map/ppermute | solution.py:20
  103.3 12.2 %collective-permute-start.13 = (f32[1,1,1024]{2,1,0:T(1,128)S(1)}, f32[1,1,1024]{2,1,0:T(1,128)S(1)}, u32[]{:S(2)}, u32[]{:S(2)}) collective-permute-start(f32[1,1,1024]{2,1,0:T(1,128)S(1)} %get-tuple-element.31), channel_id=1, source_target_pairs={{64,0},{128,64},{192,128},{256,192},{320,256},{384,320},{448,384},... | collective-permute-start | bytes 12296 | tf_op jit(solution)/shard_map/ppermute | solution.py:22
  105.3 11.5 %collective-permute-start.14 = (f32[1,1,1024]{2,1,0:T(1,128)S(1)}, f32[1,1,1024]{2,1,0:T(1,128)S(1)}, u32[]{:S(2)}, u32[]{:S(2)}) collective-permute-start(f32[1,1,1024]{2,1,0:T(1,128)S(1)} %get-tuple-element.32), channel_id=1, source_target_pairs={{0,64},{64,128},{128,192},{192,256},{256,320},{320,384},{384,448},... | collective-permute-start | bytes 12296 | tf_op jit(solution)/shard_map/ppermute | solution.py:20
  117.1 12.2 %collective-permute-start.15 = (f32[1,1,1024]{2,1,0:T(1,128)S(1)}, f32[1,1,1024]{2,1,0:T(1,128)S(1)}, u32[]{:S(2)}, u32[]{:S(2)}) collective-permute-start(f32[1,1,1024]{2,1,0:T(1,128)S(1)} %get-tuple-element.29), channel_id=1, source_target_pairs={{64,0},{128,64},{192,128},{256,192},{320,256},{384,320},{448,384},... | collective-permute-start | bytes 12296 | tf_op jit(solution)/shard_map/ppermute | solution.py:22
  119.0 11.5 %collective-permute-start.16 = (f32[1,1,1024]{2,1,0:T(1,128)S(1)}, f32[1,1,1024]{2,1,0:T(1,128)S(1)}, u32[]{:S(2)}, u32[]{:S(2)}) collective-permute-start(f32[1,1,1024]{2,1,0:T(1,128)S(1)} %get-tuple-element.30), channel_id=1, source_target_pairs={{0,64},{64,128},{128,192},{192,256},{256,320},{320,384},{384,448},... | collective-permute-start | bytes 12296 | tf_op jit(solution)/shard_map/ppermute | solution.py:20
  130.9 12.2 %collective-permute-start.17 = (f32[1,1,1024]{2,1,0:T(1,128)S(1)}, f32[1,1,1024]{2,1,0:T(1,128)S(1)}, u32[]{:S(2)}, u32[]{:S(2)}) collective-permute-start(f32[1,1,1024]{2,1,0:T(1,128)S(1)} %get-tuple-element.27), channel_id=1, source_target_pairs={{64,0},{128,64},{192,128},{256,192},{320,256},{384,320},{448,384},... | collective-permute-start | bytes 12296 | tf_op jit(solution)/shard_map/ppermute | solution.py:22
  132.8 11.5 %collective-permute-start.18 = (f32[1,1,1024]{2,1,0:T(1,128)S(1)}, f32[1,1,1024]{2,1,0:T(1,128)S(1)}, u32[]{:S(2)}, u32[]{:S(2)}) collective-permute-start(f32[1,1,1024]{2,1,0:T(1,128)S(1)} %get-tuple-element.28), channel_id=1, source_target_pairs={{0,64},{64,128},{128,192},{192,256},{256,320},{320,384},{384,448},... | collective-permute-start | bytes 12296 | tf_op jit(solution)/shard_map/ppermute | solution.py:20
  144.6 12.2 %collective-permute-start.19 = (f32[1,1,1024]{2,1,0:T(1,128)S(1)}, f32[1,1,1024]{2,1,0:T(1,128)S(1)}, u32[]{:S(2)}, u32[]{:S(2)}) collective-permute-start(f32[1,1,1024]{2,1,0:T(1,128)S(1)} %get-tuple-element.25), channel_id=1, source_target_pairs={{64,0},{128,64},{192,128},{256,192},{320,256},{384,320},{448,384},... | collective-permute-start | bytes 12296 | tf_op jit(solution)/shard_map/ppermute | solution.py:22
  146.6 11.5 %collective-permute-start.20 = (f32[1,1,1024]{2,1,0:T(1,128)S(1)}, f32[1,1,1024]{2,1,0:T(1,128)S(1)}, u32[]{:S(2)}, u32[]{:S(2)}) collective-permute-start(f32[1,1,1024]{2,1,0:T(1,128)S(1)} %get-tuple-element.26), channel_id=1, source_target_pairs={{0,64},{64,128},{128,192},{192,256},{256,320},{320,384},{384,448},... | collective-permute-start | bytes 12296 | tf_op jit(solution)/shard_map/ppermute | solution.py:20
  158.2 14.2 %copy-start.5 = (s32[1,1024]{1,0:T(1,128)S(1)}, s32[1,1024]{1,0:T(1,128)}, u32[]{:S(2)}) copy-start(s32[1,1024]{1,0:T(1,128)} %param.12) | copy-start | bytes 12292
  159.2 25.7 %all-to-all-start = ((f32[1,64,1024]{2,0,1:T(1,128)}), f32[1,64,1024]{2,0,1:T(1,128)S(1)}, u32[]{:S(2)}, u32[]{:S(2)}) async-start(f32[1,64,1024]{2,0,1:T(1,128)} %copy.274), calls=%async_computation | async-start | bytes 524288 | tf_op jit(solution)/shard_map/all_to_all | solution.py:71
  210.5 12.2 %collective-permute-start.21 = (f32[1,1,1024]{2,1,0:T(1,128)S(1)}, f32[1,1,1024]{2,1,0:T(1,128)S(1)}, u32[]{:S(2)}, u32[]{:S(2)}) collective-permute-start(f32[1,1,1024]{2,1,0:T(1,128)S(1)} %get-tuple-element.23), channel_id=1, source_target_pairs={{64,0},{128,64},{192,128},{256,192},{320,256},{384,320},{448,384},... | collective-permute-start | bytes 12296 | tf_op jit(solution)/shard_map/ppermute | solution.py:22
  212.5 11.5 %collective-permute-start.22 = (f32[1,1,1024]{2,1,0:T(1,128)S(1)}, f32[1,1,1024]{2,1,0:T(1,128)S(1)}, u32[]{:S(2)}, u32[]{:S(2)}) collective-permute-start(f32[1,1,1024]{2,1,0:T(1,128)S(1)} %get-tuple-element.24), channel_id=1, source_target_pairs={{0,64},{64,128},{128,192},{192,256},{256,320},{320,384},{384,448},... | collective-permute-start | bytes 12296 | tf_op jit(solution)/shard_map/ppermute | solution.py:20
  224.3 12.2 %collective-permute-start.23 = (f32[1,1,1024]{2,1,0:T(1,128)S(1)}, f32[1,1,1024]{2,1,0:T(1,128)S(1)}, u32[]{:S(2)}, u32[]{:S(2)}) collective-permute-start(f32[1,1,1024]{2,1,0:T(1,128)S(1)} %get-tuple-element.21), channel_id=1, source_target_pairs={{64,0},{128,64},{192,128},{256,192},{320,256},{384,320},{448,384},... | collective-permute-start | bytes 12296 | tf_op jit(solution)/shard_map/ppermute | solution.py:22
  226.2 11.5 %collective-permute-start.24 = (f32[1,1,1024]{2,1,0:T(1,128)S(1)}, f32[1,1,1024]{2,1,0:T(1,128)S(1)}, u32[]{:S(2)}, u32[]{:S(2)}) collective-permute-start(f32[1,1,1024]{2,1,0:T(1,128)S(1)} %get-tuple-element.22), channel_id=1, source_target_pairs={{0,64},{64,128},{128,192},{192,256},{256,320},{320,384},{384,448},... | collective-permute-start | bytes 12296 | tf_op jit(solution)/shard_map/ppermute | solution.py:20
  238.1 12.4 %collective-permute-start.25 = (f32[1,1,1024]{2,1,0:T(1,128)S(1)}, f32[1,1,1024]{2,1,0:T(1,128)S(1)}, u32[]{:S(2)}, u32[]{:S(2)}) collective-permute-start(f32[1,1,1024]{2,1,0:T(1,128)S(1)} %get-tuple-element.19), channel_id=1, source_target_pairs={{64,0},{128,64},{192,128},{256,192},{320,256},{384,320},{448,384},... | collective-permute-start | bytes 12296 | tf_op jit(solution)/shard_map/ppermute | solution.py:22
  240.0 11.5 %collective-permute-start.26 = (f32[1,1,1024]{2,1,0:T(1,128)S(1)}, f32[1,1,1024]{2,1,0:T(1,128)S(1)}, u32[]{:S(2)}, u32[]{:S(2)}) collective-permute-start(f32[1,1,1024]{2,1,0:T(1,128)S(1)} %get-tuple-element.20), channel_id=1, source_target_pairs={{0,64},{64,128},{128,192},{192,256},{256,320},{320,384},{384,448},... | collective-permute-start | bytes 12296 | tf_op jit(solution)/shard_map/ppermute | solution.py:20
  251.8 12.2 %collective-permute-start.27 = (f32[1,1,1024]{2,1,0:T(1,128)S(1)}, f32[1,1,1024]{2,1,0:T(1,128)S(1)}, u32[]{:S(2)}, u32[]{:S(2)}) collective-permute-start(f32[1,1,1024]{2,1,0:T(1,128)S(1)} %get-tuple-element.17), channel_id=1, source_target_pairs={{64,0},{128,64},{192,128},{256,192},{320,256},{384,320},{448,384},... | collective-permute-start | bytes 12296 | tf_op jit(solution)/shard_map/ppermute | solution.py:22
  253.8 11.5 %collective-permute-start.28 = (f32[1,1,1024]{2,1,0:T(1,128)S(1)}, f32[1,1,1024]{2,1,0:T(1,128)S(1)}, u32[]{:S(2)}, u32[]{:S(2)}) collective-permute-start(f32[1,1,1024]{2,1,0:T(1,128)S(1)} %get-tuple-element.18), channel_id=1, source_target_pairs={{0,64},{64,128},{128,192},{192,256},{256,320},{320,384},{384,448},... | collective-permute-start | bytes 12296 | tf_op jit(solution)/shard_map/ppermute | solution.py:20
  265.6 12.2 %collective-permute-start.29 = (f32[1,1,1024]{2,1,0:T(1,128)S(1)}, f32[1,1,1024]{2,1,0:T(1,128)S(1)}, u32[]{:S(2)}, u32[]{:S(2)}) collective-permute-start(f32[1,1,1024]{2,1,0:T(1,128)S(1)} %get-tuple-element.15), channel_id=1, source_target_pairs={{64,0},{128,64},{192,128},{256,192},{320,256},{384,320},{448,384},... | collective-permute-start | bytes 12296 | tf_op jit(solution)/shard_map/ppermute | solution.py:22
  267.5 11.5 %collective-permute-start.30 = (f32[1,1,1024]{2,1,0:T(1,128)S(1)}, f32[1,1,1024]{2,1,0:T(1,128)S(1)}, u32[]{:S(2)}, u32[]{:S(2)}) collective-permute-start(f32[1,1,1024]{2,1,0:T(1,128)S(1)} %get-tuple-element.16), channel_id=1, source_target_pairs={{0,64},{64,128},{128,192},{192,256},{256,320},{320,384},{384,448},... | collective-permute-start | bytes 12296 | tf_op jit(solution)/shard_map/ppermute | solution.py:20
  279.4 12.2 %collective-permute-start.31 = (f32[1,1,1024]{2,1,0:T(1,128)S(1)}, f32[1,1,1024]{2,1,0:T(1,128)S(1)}, u32[]{:S(2)}, u32[]{:S(2)}) collective-permute-start(f32[1,1,1024]{2,1,0:T(1,128)S(1)} %get-tuple-element.13), channel_id=1, source_target_pairs={{64,0},{128,64},{192,128},{256,192},{320,256},{384,320},{448,384},... | collective-permute-start | bytes 12296 | tf_op jit(solution)/shard_map/ppermute | solution.py:22
  281.3 11.5 %collective-permute-start.32 = (f32[1,1,1024]{2,1,0:T(1,128)S(1)}, f32[1,1,1024]{2,1,0:T(1,128)S(1)}, u32[]{:S(2)}, u32[]{:S(2)}) collective-permute-start(f32[1,1,1024]{2,1,0:T(1,128)S(1)} %get-tuple-element.14), channel_id=1, source_target_pairs={{0,64},{64,128},{128,192},{192,256},{256,320},{320,384},{384,448},... | collective-permute-start | bytes 12296 | tf_op jit(solution)/shard_map/ppermute | solution.py:20
  293.1 12.2 %collective-permute-start.33 = (f32[1,1,1024]{2,1,0:T(1,128)S(1)}, f32[1,1,1024]{2,1,0:T(1,128)S(1)}, u32[]{:S(2)}, u32[]{:S(2)}) collective-permute-start(f32[1,1,1024]{2,1,0:T(1,128)S(1)} %get-tuple-element.11), channel_id=1, source_target_pairs={{64,0},{128,64},{192,128},{256,192},{320,256},{384,320},{448,384},... | collective-permute-start | bytes 12296 | tf_op jit(solution)/shard_map/ppermute | solution.py:22
  295.1 11.5 %collective-permute-start.34 = (f32[1,1,1024]{2,1,0:T(1,128)S(1)}, f32[1,1,1024]{2,1,0:T(1,128)S(1)}, u32[]{:S(2)}, u32[]{:S(2)}) collective-permute-start(f32[1,1,1024]{2,1,0:T(1,128)S(1)} %get-tuple-element.12), channel_id=1, source_target_pairs={{0,64},{64,128},{128,192},{192,256},{256,320},{320,384},{384,448},... | collective-permute-start | bytes 12296 | tf_op jit(solution)/shard_map/ppermute | solution.py:20
  306.9 12.2 %collective-permute-start.35 = (f32[1,1,1024]{2,1,0:T(1,128)S(1)}, f32[1,1,1024]{2,1,0:T(1,128)S(1)}, u32[]{:S(2)}, u32[]{:S(2)}) collective-permute-start(f32[1,1,1024]{2,1,0:T(1,128)S(1)} %get-tuple-element.9), channel_id=1, source_target_pairs={{64,0},{128,64},{192,128},{256,192},{320,256},{384,320},{448,384},... | collective-permute-start | bytes 12296 | tf_op jit(solution)/shard_map/ppermute | solution.py:22
  308.8 11.5 %collective-permute-start.36 = (f32[1,1,1024]{2,1,0:T(1,128)S(1)}, f32[1,1,1024]{2,1,0:T(1,128)S(1)}, u32[]{:S(2)}, u32[]{:S(2)}) collective-permute-start(f32[1,1,1024]{2,1,0:T(1,128)S(1)} %get-tuple-element.10), channel_id=1, source_target_pairs={{0,64},{64,128},{128,192},{192,256},{256,320},{320,384},{384,448},... | collective-permute-start | bytes 12296 | tf_op jit(solution)/shard_map/ppermute | solution.py:20
  320.7 12.2 %collective-permute-start.37 = (f32[1,1,1024]{2,1,0:T(1,128)S(1)}, f32[1,1,1024]{2,1,0:T(1,128)S(1)}, u32[]{:S(2)}, u32[]{:S(2)}) collective-permute-start(f32[1,1,1024]{2,1,0:T(1,128)S(1)} %get-tuple-element.7), channel_id=1, source_target_pairs={{64,0},{128,64},{192,128},{256,192},{320,256},{384,320},{448,384},... | collective-permute-start | bytes 12296 | tf_op jit(solution)/shard_map/ppermute | solution.py:22
  322.6 11.5 %collective-permute-start.38 = (f32[1,1,1024]{2,1,0:T(1,128)S(1)}, f32[1,1,1024]{2,1,0:T(1,128)S(1)}, u32[]{:S(2)}, u32[]{:S(2)}) collective-permute-start(f32[1,1,1024]{2,1,0:T(1,128)S(1)} %get-tuple-element.8), channel_id=1, source_target_pairs={{0,64},{64,128},{128,192},{192,256},{256,320},{320,384},{384,448},... | collective-permute-start | bytes 12296 | tf_op jit(solution)/shard_map/ppermute | solution.py:20
  334.4 12.3 %collective-permute-start.39 = (f32[1,1,1024]{2,1,0:T(1,128)S(1)}, f32[1,1,1024]{2,1,0:T(1,128)S(1)}, u32[]{:S(2)}, u32[]{:S(2)}) collective-permute-start(f32[1,1,1024]{2,1,0:T(1,128)S(1)} %get-tuple-element.5), channel_id=1, source_target_pairs={{64,0},{128,64},{192,128},{256,192},{320,256},{384,320},{448,384},... | collective-permute-start | bytes 12296 | tf_op jit(solution)/shard_map/ppermute | solution.py:22
  336.4 11.7 %copy-start.4 = (f32[1,64,1024]{2,1,0:T(8,128)S(1)}, f32[1,64,1024]{2,1,0:T(8,128)}, u32[]{:S(2)}) copy-start(f32[1,64,1024]{2,1,0:T(8,128)} %param.8) | copy-start | bytes 786436
  336.4 11.7 %collective-permute-start.40 = (f32[1,1,1024]{2,1,0:T(1,128)S(1)}, f32[1,1,1024]{2,1,0:T(1,128)S(1)}, u32[]{:S(2)}, u32[]{:S(2)}) collective-permute-start(f32[1,1,1024]{2,1,0:T(1,128)S(1)} %get-tuple-element.6), channel_id=1, source_target_pairs={{0,64},{64,128},{128,192},{192,256},{256,320},{320,384},{384,448},... | collective-permute-start | bytes 12296 | tf_op jit(solution)/shard_map/ppermute | solution.py:20
where the time goes:
time: 350 us; the launch traced here: 349 us
  starting transfers between devices  266 us (76%)
  waiting for transfers between devices  45.3 us (13%)
  blocking collectives  17.4 us (5%)
  matrix products  7.53 us (2%)
  other arithmetic  6.29 us (2%)
  local copies, waits for them, and re-layouts  4.83 us (1%)
    ppermute x20, starting transfers between devices, padded(): lax.ppermute(tail, axis, [(i, (i + 1) % count) for i in range(ends)])  204 us
    ppermute x20, starting transfers between devices, padded(): lax.ppermute(head, axis, [((i + 1) % count, i) for i in range(ends)])  38.5 us
    ppermute x20, waiting for transfers between devices, padded(): lax.ppermute(tail, axis, [(i, (i + 1) % count) for i in range(ends)])  23.3 us
    all_to_all x1, blocking collectives, body(): lax.all_to_all(mixed.reshape(FIELDS * LEVELS, cell_count), 'lev', split_a...  17.4 us
    all_to_all x1, starting transfers between devices, body(): lax.all_to_all(forward.reshape(slab_count, row_count * col_count), 'lev',...  13.2 us
    all_to_all x1, waiting for transfers between devices, body(): lax.all_to_all(forward.reshape(slab_count, row_count * col_count), 'lev',...  12.4 us
    ppermute x1, starting transfers between devices, shifted(): return lax.ppermute(block, axis, route)  10.8 us
    ppermute x20, waiting for transfers between devices, padded(): lax.ppermute(head, axis, [((i + 1) % count, i) for i in range(ends)])  9.58 us
  transfers between devices with their start and end apart: 42, of which 21 were waited for; matrix products, arithmetic and copies ran while one was open for 1% of the time, Pallas kernels for 0%

commit v1 on v0

v1 whole, which is shorter than its diff:
```python
import functools

import jax
import jax.numpy as jnp
from jax import lax
from jax.experimental import pallas as pl
from jax.experimental.pallas import tpu as pltpu
from jax.sharding import PartitionSpec as P

FIELDS = 2
LEVELS = 32
STEPS = 10
REGIONS = 16
ROWS = 64
COLS = 1024
SUB = 8
LANE = 128
HALO = 10
HIGH = HALO + ROWS
ALL = HALO + ROWS + HALO
FIRST = (10,)
SECOND = (10,)
BLOCK = 14
MESH = pl.DeviceIdType.MESH
F32 = jnp.float32
BF16 = jnp.bfloat16


def rows_of(ref, start, count):
    return ref[pl.ds(SUB * start, SUB * count), :].reshape(count, SUB, LANE)


def put_rows(ref, start, value):
    count = value.shape[0]
    ref[pl.ds(SUB * start, SUB * count), :] = value.reshape(count * SUB, LANE)


def east_of(x, lane):
    near = pltpu.roll(x, LANE - 1, 2)
    return jnp.where(lane == LANE - 1, pltpu.roll(near, SUB - 1, 1), near)


def west_of(x, lane):
    near = pltpu.roll(x, 1, 2)
    return jnp.where(lane == 0, pltpu.roll(near, 1, 1), near)


def kernel(
    control_hbm, gain_hbm, north_hbm, east_hbm, land_hbm, region_hbm, tiles_hbm,
    out_ref,
    control, gain, north, east, land, region, tiles,
    base, ua, ub, ca, cn, cs, ce, cw,
    low_past, high_past, sent, got, gathered, column, mixed, returned,
    product, weights,
    in_sem, halo_send, halo_recv, late_send, late_recv, stage_send, stage_recv, region_sem, all_sem,
):
    tile = lax.axis_index("tile")
    lev = lax.axis_index("lev")
    tile_count = lax.axis_size("tile")
    which = lev // LEVELS
    mine = lax.rem(lev, LEVELS)
    last = tile_count - 1

    loads = [
        pltpu.make_async_copy(land_hbm.at[0], land, in_sem.at[0]),
        pltpu.make_async_copy(north_hbm.at[0], north, in_sem.at[1]),
        pltpu.make_async_copy(east_hbm.at[0], east, in_sem.at[2]),
        pltpu.make_async_copy(gain_hbm.at[0], gain, in_sem.at[3]),
        pltpu.make_async_copy(control_hbm.at[0], control, in_sem.at[4]),
        pltpu.make_async_copy(region_hbm, region.at[which], in_sem.at[5]),
        pltpu.make_async_copy(tiles_hbm.at[:, which], tiles, in_sem.at[6]),
    ]
    for load in loads:
        load.start()

    barrier = pltpu.get_barrier_semaphore()

    def group_peer(shift):
        return which * LEVELS + lax.rem(mine + shift, LEVELS)

    @pl.when(tile > 0)
    def _():
        pl.semaphore_signal(barrier, inc=1, device_id={"tile": tile - 1}, device_id_type=MESH)

    @pl.when(tile < last)
    def _():
        pl.semaphore_signal(barrier, inc=1, device_id={"tile": tile + 1}, device_id_type=MESH)

    partner = lax.rem(lev + LEVELS, FIELDS * LEVELS)
    pl.semaphore_signal(barrier, inc=1, device_id={"lev": partner}, device_id_type=MESH)

    def greet(shift, carry):
        pl.semaphore_signal(barrier, inc=1, device_id={"lev": group_peer(shift)}, device_id_type=MESH)
        return carry

    lax.fori_loop(1, LEVELS, greet, 0)

    for load in loads[:5]:
        load.wait()

    def relayout(block, carry):
        r = pl.multiple_of(block * SUB, SUB)
        for c in range(SUB):
            at = (pl.ds(r, SUB), slice(c * LANE, (c + 1) * LANE))
            to = pl.ds((HALO + r) * SUB + c, SUB, stride=SUB)
            ocean = land[at].astype(F32)
            base[0, to, :] = north[at]
            base[1, to, :] = east[at]
            base[2, to, :] = ocean
            start = ocean * gain[at] * control[at]
            base[3, to, :] = start
            ua[to, :] = start
        return carry

    lax.fori_loop(0, ROWS // SUB, relayout, 0)
    loads[5].wait()

    pl.semaphore_wait(barrier, LEVELS + jnp.minimum(tile, 1) + jnp.minimum(last - tile, 1))

    def rim(arrays, start, count):
        return base.at[pl.ds(0, arrays), pl.ds(SUB * start, SUB * count), :]

    def rims(arrays, near, count, send_sem, recv_sem):
        lower = pltpu.make_async_remote_copy(
            src_ref=rim(arrays, HALO + near, count), dst_ref=rim(arrays, HIGH + near, count),
            send_sem=send_sem.at[0], recv_sem=recv_sem.at[0],
            device_id={"tile": tile - 1}, device_id_type=MESH,
        )
        upper = pltpu.make_async_remote_copy(
            src_ref=rim(arrays, HIGH - near - count, count), dst_ref=rim(arrays, HALO - near - count, count),
            send_sem=send_sem.at[1], recv_sem=recv_sem.at[1],
            device_id={"tile": tile + 1}, device_id_type=MESH,
        )
        return lower, upper

    def start_both(pair):
        pl.when(tile > 0)(pair[0].start)
        pl.when(tile < last)(pair[1].start)

    def wait_both_recv(pair):
        pl.when(tile < last)(pair[0].wait_recv)
        pl.when(tile > 0)(pair[1].wait_recv)

    def wait_both_send(pair):
        pl.when(tile > 0)(pair[0].wait_send)
        pl.when(tile < last)(pair[1].wait_send)

    near = FIRST[0]
    urgent = rims(4, 0, near, halo_send, halo_recv)
    late = rims(3, near, HALO - near, late_send, late_recv) if near < HALO else None
    start_both(urgent)
    region_copy = pltpu.make_async_remote_copy(
        src_ref=region.at[which], dst_ref=region.at[which],
        send_sem=region_sem.at[0], recv_sem=region_sem.at[1],
        device_id={"lev": partner}, device_id_type=MESH,
    )
    region_copy.start()

    @pl.when(tile == 0)
    def _():
        for a in range(4):
            base[a, : SUB * HALO, :] = jnp.zeros((SUB * HALO, LANE), F32)
        for g in got:
            g[0] = jnp.zeros(g.shape[1:], F32)

    @pl.when(tile == last)
    def _():
        for a in range(4):
            base[a, SUB * HIGH :, :] = jnp.zeros((SUB * HALO, LANE), F32)
        for g in got:
            g[1] = jnp.zeros(g.shape[1:], F32)

    loads[6].wait()

    def square(r, carry):
        t = tiles[r]
        m = lax.dot_general(
            t, t, (((0,), (0,)), ((), ())), precision=lax.Precision.HIGHEST, preferred_element_type=F32
        )
        product[pl.ds(pl.multiple_of(r * LEVELS, LEVELS), LEVELS), :] = m
        return carry

    lax.fori_loop(0, REGIONS, square, 0)

    def thirds(x):
        one = x.astype(BF16)
        rest = x - one.astype(F32)
        two = rest.astype(BF16)
        three = (rest - two.astype(F32)).astype(BF16)
        return one, two, three

    k_of = lax.broadcasted_iota(jnp.int32, (LEVELS, 6 * LEVELS), 0)
    j_of = lax.broadcasted_iota(jnp.int32, (LEVELS, 6 * LEVELS), 1)
    total = None
    for part, groups in zip(thirds(product[...]), ((0, 1, 3), (2, 4), (5,))):
        pick = jnp.zeros((LEVELS, 6 * LEVELS), F32)
        for g in groups:
            pick = pick + jnp.where(j_of == k_of + g * LEVELS, 1.0, 0.0)
        spread = jnp.dot(part, pick.astype(BF16), preferred_element_type=F32)
        total = spread if total is None else total + spread
    weights[...] = total.astype(BF16)

    first_lane = (1, SUB, LANE)
    lane1 = lax.broadcasted_iota(jnp.int32, first_lane, 2)
    sub1 = lax.broadcasted_iota(jnp.int32, first_lane, 1)
    west_edge = jnp.logical_and(lane1 == 0, sub1 == 0)
    east_edge = jnp.logical_and(lane1 == LANE - 1, sub1 == SUB - 1)

    def make_coef(start, count):
        shape = (count, SUB, LANE)
        lane = jnp.broadcast_to(lane1, shape)
        n = rows_of(base.at[0], start, count)
        s = rows_of(base.at[0], start - 1, count)
        e = rows_of(base.at[1], start, count)
        o = rows_of(base.at[2], start, count)
        w = jnp.where(west_edge, 0.0, west_of(e, lane))
        put_rows(ca, start, o * (1.0 - n - s - e - w))
        put_rows(cn, start, o * n)
        put_rows(cs, start, o * s)
        put_rows(ce, start, o * jnp.where(east_edge, 0.0, e))
        put_rows(cw, start, o * w)

    def coefs(start, end):
        for at in range(start, end, BLOCK):
            make_coef(at, min(BLOCK, end - at))

    def coef_block(b, carry):
        make_coef(HALO + 1 + b * 9, 9)
        return carry

    lax.fori_loop(0, (ROWS - 1) // 9, coef_block, 0)

    def advance(wide, start, count):
        lane = jnp.broadcast_to(lane1, (count, SUB, LANE))
        u = wide[1:-1]
        v = rows_of(ca, start, count) * u
        v = v + rows_of(cn, start, count) * wide[2:]
        v = v + rows_of(cs, start, count) * wide[:-2]
        v = v + rows_of(ce, start, count) * east_of(u, lane)
        return v + rows_of(cw, start, count) * west_of(u, lane)

    def inner_step(src, dst, s):
        low_past[s] = src[pl.ds(SUB * (HALO + s), 2 * SUB), :]
        high_past[s] = src[pl.ds(SUB * (HIGH - 2 - s), 2 * SUB), :]
        at, end = HALO + 1, HIGH - 1
        while at < end:
            count = min(BLOCK, end - at)
            put_rows(dst, at, advance(rows_of(src, at - 1, count + 2), at, count))
            at += count

    def inner(src, other, depth):
        def pair(i, carry):
            inner_step(src, other, 2 * i)
            inner_step(other, src, 2 * i + 1)
            return carry

        if depth // 2:
            lax.fori_loop(0, depth // 2, pair, 0)
        if depth % 2:
            inner_step(src, other, depth - 1)
            return other, src
        return src, other

    def outer(dst, low, high, depth):
        def one(s, carry):
            low, high = carry
            past = low_past[s].reshape(2, SUB, LANE)
            low = advance(jnp.concatenate([low, past], axis=0), HALO - depth + 1 + s, depth)
            past = high_past[s].reshape(2, SUB, LANE)
            high = advance(jnp.concatenate([past, high], axis=0), HIGH - 1 - s, depth)
            return low, high

        low, high = lax.fori_loop(0, depth, one, (low, high))
        put_rows(dst, HALO, low)
        put_rows(dst, HIGH - depth, high)

    def swap(field, depth, number):
        sent[number][0] = field[SUB * HALO : SUB * (HALO + depth), :]
        sent[number][1] = field[SUB * (HIGH - depth) : SUB * HIGH, :]
        lower = pltpu.make_async_remote_copy(
            src_ref=sent[number].at[0], dst_ref=got[number].at[1],
            send_sem=stage_send.at[number, 0], recv_sem=stage_recv.at[number, 0],
            device_id={"tile": tile - 1}, device_id_type=MESH,
        )
        upper = pltpu.make_async_remote_copy(
            src_ref=sent[number].at[1], dst_ref=got[number].at[0],
            send_sem=stage_send.at[number, 1], recv_sem=stage_recv.at[number, 1],
            device_id={"tile": tile + 1}, device_id_type=MESH,
        )
        start_both((lower, upper))
        return lower, upper

    swaps = []
    field, other = ua, ub
    for stage, depth in enumerate(FIRST):
        if stage:
            swaps.append(swap(field, depth, len(swaps)))
            if stage == 1:
                start_both(late)
        field, other = inner(field, other, depth)
        if stage:
            wait_both_recv(swaps[-1])
            low, high = (g.reshape(depth, SUB, LANE) for g in (got[len(swaps) - 1][0], got[len(swaps) - 1][1]))
        else:
            wait_both_recv(urgent)
            coefs(HALO - near + 1, HALO + 1)
            coefs(HIGH, HIGH + near - 1)
            low = rows_of(base.at[3], HALO - depth, depth)
            high = rows_of(base.at[3], HIGH, depth)
        outer(field, low, high, depth)

    for h in range(2):
        gathered[h] = rows_of(field, HALO + h * LEVELS, LEVELS)

    def to_columns(shift, carry):
        peer = lax.rem(mine + shift, LEVELS)
        pltpu.make_async_remote_copy(
            src_ref=gathered.at[:, peer], dst_ref=column.at[:, mine],
            send_sem=all_sem.at[0], recv_sem=all_sem.at[1],
            device_id={"lev": which * LEVELS + peer}, device_id_type=MESH,
        ).start()
        return carry

    pltpu.make_async_copy(gathered.at[:, mine], column.at[:, mine], all_sem.at[1]).start()
    lax.fori_loop(1, LEVELS, to_columns, 0)

    def wait_all(ref, sem):
        pltpu.make_async_copy(ref, ref, sem).wait()

    region_copy.wait()
    wait_all(column, all_sem.at[1])

    wide = 2 * LANE
    column2 = column.reshape(2 * LEVELS * SUB, LANE)
    mixed2 = mixed.reshape(2 * LEVELS * SUB, LANE)

    def mix(i, carry):
        h = i // (SUB // 2)
        c = 2 * lax.rem(i, SUB // 2)
        start = h * LEVELS * SUB + c
        x = jnp.concatenate(
            [column2[pl.ds(start + q, LEVELS, stride=SUB), :] for q in range(2)], axis=1
        )
        one, two, three = thirds(x)
        stacked = jnp.concatenate([one, two, one, three, two, one], axis=0)
        every = jnp.dot(weights[...], stacked, preferred_element_type=F32)
        ids = region[h, :, pl.ds(pl.multiple_of(c * LANE, wide), wide)]
        ids = jnp.broadcast_to(ids, (LEVELS, wide))
        y = every[:LEVELS]
        for r in range(1, REGIONS):
            y = jnp.where(ids == r, every[r * LEVELS : (r + 1) * LEVELS], y)
        for q in range(2):
            mixed2[pl.ds(start + q, LEVELS, stride=SUB), :] = y[:, q * LANE : (q + 1) * LANE]
        return carry

    lax.fori_loop(0, SUB, mix, 0)

    def to_levels(shift, carry):
        peer = lax.rem(mine + shift, LEVELS)
        pltpu.make_async_remote_copy(
            src_ref=mixed.at[:, peer], dst_ref=returned.at[:, mine],
            send_sem=all_sem.at[2], recv_sem=all_sem.at[3],
            device_id={"lev": which * LEVELS + peer}, device_id_type=MESH,
        ).start()
        return carry

    pltpu.make_async_copy(mixed.at[:, mine], returned.at[:, mine], all_sem.at[3]).start()
    lax.fori_loop(1, LEVELS, to_levels, 0)
    wait_all(returned, all_sem.at[3])

    field, other = ua, ub
    for h in range(2):
        o = rows_of(base.at[2], HALO + h * LEVELS, LEVELS)
        put_rows(field, HALO + h * LEVELS, o * returned[h])

    for stage, depth in enumerate(SECOND):
        swaps.append(swap(field, depth, len(swaps)))
        field, other = inner(field, other, depth)
        if stage == 0 and late is not None:
            wait_both_recv(late)
            coefs(1, HALO - near + 1)
            coefs(HIGH + near - 1, ALL - 1)
        wait_both_recv(swaps[-1])
        low, high = (g.reshape(depth, SUB, LANE) for g in (got[len(swaps) - 1][0], got[len(swaps) - 1][1]))
        outer(field, low, high, depth)

    def finish(block, carry):
        r = pl.multiple_of(block * SUB, SUB)
        for c in range(SUB):
            at = (pl.ds(r, SUB), slice(c * LANE, (c + 1) * LANE))
            out_ref[at] = gain[at] * field[pl.ds((HALO + r) * SUB + c, SUB, stride=SUB), :]
        return carry

    lax.fori_loop(0, ROWS // SUB, finish, 0)

    def sends(ref, sem):
        part = ref.at[:, pl.ds(0, LEVELS - 1)]
        pltpu.make_async_copy(part, part, sem).wait()

    sends(gathered, all_sem.at[0])
    sends(mixed, all_sem.at[2])
    wait_both_send(urgent)
    if late is not None:
        wait_both_send(late)
    for pair in swaps:
        wait_both_send(pair)


def body(*args):
    raw = pltpu.VMEM((ROWS, COLS), F32)
    field = pltpu.VMEM((ALL * SUB, LANE), F32)
    depths = FIRST[1:] + SECOND
    slots = [pltpu.VMEM((2, d * SUB, LANE), F32) for d in depths]
    cube = pltpu.VMEM((2, LEVELS, SUB, LANE), F32)
    out = pl.pallas_call(
        kernel,
        out_shape=jax.ShapeDtypeStruct((ROWS, COLS), F32),
        in_specs=[pl.BlockSpec(memory_space=pltpu.HBM)] * 7,
        out_specs=pl.BlockSpec(memory_space=pltpu.VMEM),
        scratch_shapes=[
            raw, raw, raw, raw,
            pltpu.VMEM((ROWS, COLS), jnp.int32),
            pltpu.VMEM((2, 1, COLS), jnp.int32),
            pltpu.VMEM((REGIONS, LEVELS, LEVELS), F32),
            pltpu.VMEM((4, ALL * SUB, LANE), F32),
            field, field, field, field, field, field, field,
            pltpu.VMEM((HALO, 2 * SUB, LANE), F32),
            pltpu.VMEM((HALO, 2 * SUB, LANE), F32),
            slots, slots,
            cube, cube, cube, cube,
            pltpu.VMEM((REGIONS * LEVELS, LEVELS), F32),
            pltpu.VMEM((REGIONS * LEVELS, 6 * LEVELS), BF16),
            pltpu.SemaphoreType.DMA((7,)),
            pltpu.SemaphoreType.DMA((2,)),
            pltpu.SemaphoreType.DMA((2,)),
            pltpu.SemaphoreType.DMA((2,)),
            pltpu.SemaphoreType.DMA((2,)),
            pltpu.SemaphoreType.DMA((len(depths), 2)),
            pltpu.SemaphoreType.DMA((len(depths), 2)),
            pltpu.SemaphoreType.DMA((2,)),
            pltpu.SemaphoreType.DMA((4,)),
        ],
        compiler_params=pltpu.CompilerParams(
            collective_id=0, has_side_effects=True, vmem_limit_bytes=32 * 1024 * 1024
        ),
        name="covariance",
    )(*[pltpu.with_memory_space_constraint(x, pltpu.HBM) for x in args])
    return out[None]


def solution(mesh):
    return jax.shard_map(
        body,
        mesh=mesh,
        in_specs=(
            P("lev", "tile", None),
            P("lev", "tile", None),
            P("lev", "tile", None),
            P("lev", "tile", None),
            P("lev", "tile", None),
            P(("tile", "lev"), None),
            P(),
        ),
        out_specs=P("lev", "tile", None),
        check_vma=False,
    )
```

time: 350 us -> 55.9 us (0.16)
  the two profiles are of different devices: /device:TPU:6 before, /device:TPU:68 now
where the time goes in v1:
time: 55.9 us; the launch traced here: 55.8 us
  Pallas kernels  55 us (98%)
  local copies, waits for them, and re-layouts  0.71 us (1%)
    pallas_call x1, Pallas kernels, body(): pl.pallas_call(kernel, out_shape=jax.ShapeDtypeStruct((ROWS, COLS), F32),...  55 us

profile of v1, /device:TPU:68, one launch (start us, length us, event | category | flops | bytes accessed | tf_op | source)
XLA Modules:
  0.0 55.8 jit_solution(12296869612916902023)
XLA Ops:
  0.0 55.0 %covariance.1 = f32[64,1024]{1,0:T(8,128)S(1)} custom-call(f32[1,64,1024]{2,1,0:T(8,128)} %control_hbm.1, f32[1,64,1024]{2,1,0:T(8,128)} %gain_hbm.1, f32[1,64,1024]{2,1,0:T(8,128)} %north_hbm.1, f32[1,64,1024]{2,1,0:T(8,128)} %east_hbm.1, s32[1,64,1024]{2,1,0:T(8,128)} %land_hbm.1, s32[1,1024]{1,0:T(1,128)} %region_hbm.1, f32[16,2,32,32]{3,2,1,0:T(8,128)} %tiles_hbm.1), custom_call_target="tpu_custom_call" | custom-call | tf_op jit(solution)/shard_map/covariance/pallas_call | solution.py:415
  55.1 0.7 %copy.9 = f32[1,64,1024]{2,1,0:T(8,128)} copy(f32[1,64,1024]{2,1,0:T(8,128)S(1)} %bitcast.1) | data formatting | bytes 524288

commit v2 on v1

--- a/solution.py
+++ b/solution.py
@@ -18,8 +18,7 @@
 HALO = 10
 HIGH = HALO + ROWS
 ALL = HALO + ROWS + HALO
-FIRST = (10,)
-SECOND = (10,)
+WIDE = 4
 BLOCK = 14
 MESH = pl.DeviceIdType.MESH
 F32 = jnp.float32
@@ -50,9 +49,9 @@
     out_ref,
     control, gain, north, east, land, region, tiles,
     base, ua, ub, ca, cn, cs, ce, cw,
-    low_past, high_past, sent, got, gathered, column, mixed, returned,
+    low_past, high_past, carried, sent, got, gathered, column, mixed, returned,
     product, weights,
-    in_sem, halo_send, halo_recv, late_send, late_recv, stage_send, stage_recv, region_sem, all_sem,
+    in_sem, halo_send, halo_recv, carry_recv, carry_send, swap_send, swap_recv, region_sem, all_sem,
 ):
     tile = lax.axis_index("tile")
     lev = lax.axis_index("lev")
@@ -60,6 +59,13 @@
     which = lev // LEVELS
     mine = lax.rem(lev, LEVELS)
     last = tile_count - 1
+    place = lax.rem(tile, WIDE)
+    band = tile // WIDE
+    bands = tile_count // WIDE
+    upper_end = jnp.logical_and(place == WIDE - 1, band < bands - 1)
+    lower_end = jnp.logical_and(place == 0, band > 0)
+    down_carrier = jnp.logical_and(place > 0, band > 0)
+    up_carrier = jnp.logical_and(place < WIDE - 1, band < bands - 1)
 
     loads = [
         pltpu.make_async_copy(land_hbm.at[0], land, in_sem.at[0]),
@@ -85,6 +91,20 @@
     @pl.when(tile < last)
     def _():
         pl.semaphore_signal(barrier, inc=1, device_id={"tile": tile + 1}, device_id_type=MESH)
+
+    for far in range(1, WIDE):
+        for end, offset in ((upper_end, far + 1), (lower_end, far), (lower_end, -far - 1), (upper_end, -far)):
+            @pl.when(end)
+            def _(offset=offset):
+                pl.semaphore_signal(barrier, inc=1, device_id={"tile": tile + offset}, device_id_type=MESH)
+
+    for carrier, offset in (
+        (down_carrier, -place - 1), (down_carrier, -place),
+        (up_carrier, WIDE - place), (up_carrier, WIDE - 1 - place),
+    ):
+        @pl.when(carrier)
+        def _(offset=offset):
+            pl.semaphore_signal(barrier, inc=1, device_id={"tile": tile + offset}, device_id_type=MESH)
 
     partner = lax.rem(lev + LEVELS, FIELDS * LEVELS)
     pl.semaphore_signal(barrier, inc=1, device_id={"lev": partner}, device_id_type=MESH)
@@ -115,40 +135,64 @@
     lax.fori_loop(0, ROWS // SUB, relayout, 0)
     loads[5].wait()
 
-    pl.semaphore_wait(barrier, LEVELS + jnp.minimum(tile, 1) + jnp.minimum(last - tile, 1))
-
-    def rim(arrays, start, count):
-        return base.at[pl.ds(0, arrays), pl.ds(SUB * start, SUB * count), :]
-
-    def rims(arrays, near, count, send_sem, recv_sem):
-        lower = pltpu.make_async_remote_copy(
-            src_ref=rim(arrays, HALO + near, count), dst_ref=rim(arrays, HIGH + near, count),
-            send_sem=send_sem.at[0], recv_sem=recv_sem.at[0],
-            device_id={"tile": tile - 1}, device_id_type=MESH,
+    def as_count(flag):
+        return flag.astype(jnp.int32)
+
+    greeted = LEVELS + as_count(tile > 0) + as_count(tile < last)
+    greeted = greeted + 2 * (WIDE - 1) * (as_count(upper_end) + as_count(lower_end))
+    greeted = greeted + 2 * (as_count(up_carrier) + as_count(down_carrier))
+    pl.semaphore_wait(barrier, greeted)
+
+    def rim(a, start):
+        return base.at[a, pl.ds(SUB * start, SUB * HALO), :]
+
+    def send_rim(a, side, offset, to=None):
+        start, land_at = ((HALO, HIGH), (HIGH - HALO, 0))[side]
+        return pltpu.make_async_remote_copy(
+            src_ref=rim(a, start), dst_ref=rim(a, land_at) if to is None else to,
+            send_sem=halo_send.at[side, a],
+            recv_sem=halo_recv.at[side, a] if to is None else carry_recv.at[side],
+            device_id={"tile": tile + offset}, device_id_type=MESH,
         )
-        upper = pltpu.make_async_remote_copy(
-            src_ref=rim(arrays, HIGH - near - count, count), dst_ref=rim(arrays, HALO - near - count, count),
-            send_sem=send_sem.at[1], recv_sem=recv_sem.at[1],
-            device_id={"tile": tile + 1}, device_id_type=MESH,
+
+    def forward(side):
+        a = (place - 1, WIDE - 2 - place)[side]
+        return pltpu.make_async_remote_copy(
+            src_ref=carried.at[side], dst_ref=rim(a, (HIGH, 0)[side]),
+            send_sem=carry_send.at[side], recv_sem=halo_recv.at[side, a],
+            device_id={"tile": tile + (-place - 1, WIDE - place)[side]}, device_id_type=MESH,
         )
-        return lower, upper
+
+    has_lower, has_upper = tile > 0, tile < last
 
     def start_both(pair):
-        pl.when(tile > 0)(pair[0].start)
-        pl.when(tile < last)(pair[1].start)
+        pl.when(has_lower)(pair[0].start)
+        pl.when(has_upper)(pair[1].start)
 
     def wait_both_recv(pair):
-        pl.when(tile < last)(pair[0].wait_recv)
-        pl.when(tile > 0)(pair[1].wait_recv)
+        pl.when(has_upper)(pair[0].wait_recv)
+        pl.when(has_lower)(pair[1].wait_recv)
 
     def wait_both_send(pair):
-        pl.when(tile > 0)(pair[0].wait_send)
-        pl.when(tile < last)(pair[1].wait_send)
-
-    near = FIRST[0]
-    urgent = rims(4, 0, near, halo_send, halo_recv)
-    late = rims(3, near, HALO - near, late_send, late_recv) if near < HALO else None
-    start_both(urgent)
+        pl.when(has_lower)(pair[0].wait_send)
+        pl.when(has_upper)(pair[1].wait_send)
+
+    straight = [(send_rim(a, 0, -1), send_rim(a, 1, 1)) for a in range(4)]
+    for a in range(WIDE - 1):
+        pl.when(lower_end)(send_rim(a, 0, 1 + a, carried.at[0]).start)
+        pl.when(upper_end)(send_rim(a, 1, -1 - a, carried.at[1]).start)
+        pl.when(jnp.logical_and(has_lower, jnp.logical_not(lower_end)))(straight[a][0].start)
+        pl.when(jnp.logical_and(has_upper, jnp.logical_not(upper_end)))(straight[a][1].start)
+    start_both(straight[3])
+
+    def carry_on():
+        for side, carrier in enumerate((down_carrier, up_carrier)):
+            @pl.when(carrier)
+            def _(side=side):
+                copy = forward(side)
+                pltpu.make_async_copy(carried.at[side], carried.at[side], carry_recv.at[side]).wait()
+                copy.start()
+
     region_copy = pltpu.make_async_remote_copy(
         src_ref=region.at[which], dst_ref=region.at[which],
         send_sem=region_sem.at[0], recv_sem=region_sem.at[1],
@@ -160,15 +204,13 @@
     def _():
         for a in range(4):
             base[a, : SUB * HALO, :] = jnp.zeros((SUB * HALO, LANE), F32)
-        for g in got:
-            g[0] = jnp.zeros(g.shape[1:], F32)
+        got[0] = jnp.zeros(got.shape[1:], F32)
 
     @pl.when(tile == last)
     def _():
         for a in range(4):
             base[a, SUB * HIGH :, :] = jnp.zeros((SUB * HALO, LANE), F32)
-        for g in got:
-            g[1] = jnp.zeros(g.shape[1:], F32)
+        got[1] = jnp.zeros(got.shape[1:], F32)
 
     loads[6].wait()
 
@@ -248,87 +290,57 @@
             put_rows(dst, at, advance(rows_of(src, at - 1, count + 2), at, count))
             at += count
 
-    def inner(src, other, depth):
+    def inner():
         def pair(i, carry):
-            inner_step(src, other, 2 * i)
-            inner_step(other, src, 2 * i + 1)
+            inner_step(ua, ub, 2 * i)
+            inner_step(ub, ua, 2 * i + 1)
             return carry
 
-        if depth // 2:
-            lax.fori_loop(0, depth // 2, pair, 0)
-        if depth % 2:
-            inner_step(src, other, depth - 1)
-            return other, src
-        return src, other
-
-    def outer(dst, low, high, depth):
+        lax.fori_loop(0, STEPS // 2, pair, 0)
+
+    def outer(low, high):
         def one(s, carry):
             low, high = carry
             past = low_past[s].reshape(2, SUB, LANE)
-            low = advance(jnp.concatenate([low, past], axis=0), HALO - depth + 1 + s, depth)
+            low = advance(jnp.concatenate([low, past], axis=0), 1 + s, HALO)
             past = high_past[s].reshape(2, SUB, LANE)
-            high = advance(jnp.concatenate([past, high], axis=0), HIGH - 1 - s, depth)
+            high = advance(jnp.concatenate([past, high], axis=0), HIGH - 1 - s, HALO)
             return low, high
 
-        low, high = lax.fori_loop(0, depth, one, (low, high))
-        put_rows(dst, HALO, low)
-        put_rows(dst, HIGH - depth, high)
-
-    def swap(field, depth, number):
-        sent[number][0] = field[SUB * HALO : SUB * (HALO + depth), :]
-        sent[number][1] = field[SUB * (HIGH - depth) : SUB * HIGH, :]
-        lower = pltpu.make_async_remote_copy(
-            src_ref=sent[number].at[0], dst_ref=got[number].at[1],
-            send_sem=stage_send.at[number, 0], recv_sem=stage_recv.at[number, 0],
-            device_id={"tile": tile - 1}, device_id_type=MESH,
-        )
-        upper = pltpu.make_async_remote_copy(
-            src_ref=sent[number].at[1], dst_ref=got[number].at[0],
-            send_sem=stage_send.at[number, 1], recv_sem=stage_recv.at[number, 1],
-            device_id={"tile": tile + 1}, device_id_type=MESH,
-        )
-        start_both((lower, upper))
-        return lower, upper
-
-    swaps = []
-    field, other = ua, ub
-    for stage, depth in enumerate(FIRST):
-        if stage:
-            swaps.append(swap(field, depth, len(swaps)))
-            if stage == 1:
-                start_both(late)
-        field, other = inner(field, other, depth)
-        if stage:
-            wait_both_recv(swaps[-1])
-            low, high = (g.reshape(depth, SUB, LANE) for g in (got[len(swaps) - 1][0], got[len(swaps) - 1][1]))
-        else:
-            wait_both_recv(urgent)
-            coefs(HALO - near + 1, HALO + 1)
-            coefs(HIGH, HIGH + near - 1)
-            low = rows_of(base.at[3], HALO - depth, depth)
-            high = rows_of(base.at[3], HIGH, depth)
-        outer(field, low, high, depth)
+        low, high = lax.fori_loop(0, STEPS, one, (low, high))
+        put_rows(ua, HALO, low)
+        put_rows(ua, HIGH - HALO, high)
+
+    carry_on()
+    inner()
+    for pair in straight:
+        wait_both_recv(pair)
+    coefs(1, HALO + 1)
+    coefs(HIGH, ALL - 1)
+    outer(rows_of(base.at[3], 0, HALO), rows_of(base.at[3], HIGH, HALO))
 
     for h in range(2):
-        gathered[h] = rows_of(field, HALO + h * LEVELS, LEVELS)
-
-    def to_columns(shift, carry):
-        peer = lax.rem(mine + shift, LEVELS)
-        pltpu.make_async_remote_copy(
-            src_ref=gathered.at[:, peer], dst_ref=column.at[:, mine],
-            send_sem=all_sem.at[0], recv_sem=all_sem.at[1],
-            device_id={"lev": which * LEVELS + peer}, device_id_type=MESH,
-        ).start()
-        return carry
-
-    pltpu.make_async_copy(gathered.at[:, mine], column.at[:, mine], all_sem.at[1]).start()
-    lax.fori_loop(1, LEVELS, to_columns, 0)
-
-    def wait_all(ref, sem):
-        pltpu.make_async_copy(ref, ref, sem).wait()
-
+        gathered[h] = rows_of(ua, HALO + h * LEVELS, LEVELS)
+
+    def regroup(src, dst, h, sems):
+        def one(shift, carry):
+            peer = lax.rem(mine + shift, LEVELS)
+            pltpu.make_async_remote_copy(
+                src_ref=src.at[h, peer], dst_ref=dst.at[h, mine],
+                send_sem=sems.at[0, h], recv_sem=sems.at[1, h],
+                device_id={"lev": which * LEVELS + peer}, device_id_type=MESH,
+            ).start()
+            return carry
+
+        pltpu.make_async_copy(src.at[h, mine], dst.at[h, mine], sems.at[1, h]).start()
+        lax.fori_loop(1, LEVELS, one, 0)
+
+    def wait_half(ref, h, sem):
+        pltpu.make_async_copy(ref.at[h], ref.at[h], sem).wait()
+
+    for h in range(2):
+        regroup(gathered, column, h, all_sem.at[0])
     region_copy.wait()
-    wait_all(column, all_sem.at[1])
 
     wide = 2 * LANE
     column2 = column.reshape(2 * LEVELS * SUB, LANE)
@@ -353,64 +365,56 @@
             mixed2[pl.ds(start + q, LEVELS, stride=SUB), :] = y[:, q * LANE : (q + 1) * LANE]
         return carry
 
-    lax.fori_loop(0, SUB, mix, 0)
-
-    def to_levels(shift, carry):
-        peer = lax.rem(mine + shift, LEVELS)
-        pltpu.make_async_remote_copy(
-            src_ref=mixed.at[:, peer], dst_ref=returned.at[:, mine],
-            send_sem=all_sem.at[2], recv_sem=all_sem.at[3],
-            device_id={"lev": which * LEVELS + peer}, device_id_type=MESH,
-        ).start()
-        return carry
-
-    pltpu.make_async_copy(mixed.at[:, mine], returned.at[:, mine], all_sem.at[3]).start()
-    lax.fori_loop(1, LEVELS, to_levels, 0)
-    wait_all(returned, all_sem.at[3])
-
-    field, other = ua, ub
+    for h in range(2):
+        wait_half(column, h, all_sem.at[0, 1, h])
+        lax.fori_loop(h * SUB // 2, (h + 1) * SUB // 2, mix, 0)
+        regroup(mixed, returned, h, all_sem.at[1])
+    for h in range(2):
+        wait_half(returned, h, all_sem.at[1, 1, h])
+
     for h in range(2):
         o = rows_of(base.at[2], HALO + h * LEVELS, LEVELS)
-        put_rows(field, HALO + h * LEVELS, o * returned[h])
-
-    for stage, depth in enumerate(SECOND):
-        swaps.append(swap(field, depth, len(swaps)))
-        field, other = inner(field, other, depth)
-        if stage == 0 and late is not None:
-            wait_both_recv(late)
-            coefs(1, HALO - near + 1)
-            coefs(HIGH + near - 1, ALL - 1)
-        wait_both_recv(swaps[-1])
-        low, high = (g.reshape(depth, SUB, LANE) for g in (got[len(swaps) - 1][0], got[len(swaps) - 1][1]))
-        outer(field, low, high, depth)
+        put_rows(ua, HALO + h * LEVELS, o * returned[h])
+
+    sent[0] = ua[SUB * HALO : 2 * SUB * HALO, :]
+    sent[1] = ua[SUB * (HIGH - HALO) : SUB * HIGH, :]
+    swap = tuple(
+        pltpu.make_async_remote_copy(
+            src_ref=sent.at[side], dst_ref=got.at[1 - side],
+            send_sem=swap_send.at[side], recv_sem=swap_recv.at[side],
+            device_id={"tile": tile + 2 * side - 1}, device_id_type=MESH,
+        )
+        for side in range(2)
+    )
+    start_both(swap)
+    inner()
+    wait_both_recv(swap)
+    outer(got[0].reshape(HALO, SUB, LANE), got[1].reshape(HALO, SUB, LANE))
 
     def finish(block, carry):
         r = pl.multiple_of(block * SUB, SUB)
         for c in range(SUB):
             at = (pl.ds(r, SUB), slice(c * LANE, (c + 1) * LANE))
-            out_ref[at] = gain[at] * field[pl.ds((HALO + r) * SUB + c, SUB, stride=SUB), :]
+            out_ref[at] = gain[at] * ua[pl.ds((HALO + r) * SUB + c, SUB, stride=SUB), :]
         return carry
 
     lax.fori_loop(0, ROWS // SUB, finish, 0)
 
-    def sends(ref, sem):
-        part = ref.at[:, pl.ds(0, LEVELS - 1)]
-        pltpu.make_async_copy(part, part, sem).wait()
-
-    sends(gathered, all_sem.at[0])
-    sends(mixed, all_sem.at[2])
-    wait_both_send(urgent)
-    if late is not None:
-        wait_both_send(late)
-    for pair in swaps:
+    for ref, sems in ((gathered, all_sem.at[0]), (mixed, all_sem.at[1])):
+        for h in range(2):
+            part = ref.at[h, pl.ds(0, LEVELS - 1)]
+            pltpu.make_async_copy(part, part, sems.at[0, h]).wait()
+    for pair in straight:
         wait_both_send(pair)
+    wait_both_send(swap)
+    for side, carrier in enumerate((down_carrier, up_carrier)):
+        pl.when(carrier)(forward(side).wait_send)
 
 
 def body(*args):
     raw = pltpu.VMEM((ROWS, COLS), F32)
     field = pltpu.VMEM((ALL * SUB, LANE), F32)
-    depths = FIRST[1:] + SECOND
-    slots = [pltpu.VMEM((2, d * SUB, LANE), F32) for d in depths]
+    slots = pltpu.VMEM((2, HALO * SUB, LANE), F32)
     cube = pltpu.VMEM((2, LEVELS, SUB, LANE), F32)
     out = pl.pallas_call(
         kernel,
@@ -426,19 +430,19 @@
             field, field, field, field, field, field, field,
             pltpu.VMEM((HALO, 2 * SUB, LANE), F32),
             pltpu.VMEM((HALO, 2 * SUB, LANE), F32),
-            slots, slots,
+            slots, slots, slots,
             cube, cube, cube, cube,
             pltpu.VMEM((REGIONS * LEVELS, LEVELS), F32),
             pltpu.VMEM((REGIONS * LEVELS, 6 * LEVELS), BF16),
             pltpu.SemaphoreType.DMA((7,)),
+            pltpu.SemaphoreType.DMA((2, 4)),
+            pltpu.SemaphoreType.DMA((2, 4)),
             pltpu.SemaphoreType.DMA((2,)),
             pltpu.SemaphoreType.DMA((2,)),
             pltpu.SemaphoreType.DMA((2,)),
             pltpu.SemaphoreType.DMA((2,)),
-            pltpu.SemaphoreType.DMA((len(depths), 2)),
-            pltpu.SemaphoreType.DMA((len(depths), 2)),
             pltpu.SemaphoreType.DMA((2,)),
-            pltpu.SemaphoreType.DMA((4,)),
+            pltpu.SemaphoreType.DMA((2, 2, 2)),
         ],
         compiler_params=pltpu.CompilerParams(
             collective_id=0, has_side_effects=True, vmem_limit_bytes=32 * 1024 * 1024

time: 55.9 us -> 50.7 us (0.907)
  the two profiles are of different devices: /device:TPU:68 before, /device:TPU:6 now
where the time goes in v2:
time: 50.7 us; the launch traced here: 50.4 us
  Pallas kernels  49.7 us (98%)
  local copies, waits for them, and re-layouts  0.71 us (1%)
    pallas_call x1, Pallas kernels, body(): pl.pallas_call(kernel, out_shape=jax.ShapeDtypeStruct((ROWS, COLS), F32),...  49.7 us

profile of v2, /device:TPU:6, one launch (start us, length us, event | category | flops | bytes accessed | tf_op | source)
XLA Modules:
  0.0 50.4 jit_solution(13400674097409895189)
XLA Ops:
  0.0 49.7 %covariance.1 = f32[64,1024]{1,0:T(8,128)S(1)} custom-call(f32[1,64,1024]{2,1,0:T(8,128)} %control_hbm.1, f32[1,64,1024]{2,1,0:T(8,128)} %gain_hbm.1, f32[1,64,1024]{2,1,0:T(8,128)} %north_hbm.1, f32[1,64,1024]{2,1,0:T(8,128)} %east_hbm.1, s32[1,64,1024]{2,1,0:T(8,128)} %land_hbm.1, s32[1,1024]{1,0:T(1,128)} %region_hbm.1, f32[16,2,32,32]{3,2,1,0:T(8,128)} %tiles_hbm.1), custom_call_target="tpu_custom_call" | custom-call | tf_op jit(solution)/shard_map/covariance/pallas_call | solution.py:419
  49.7 0.7 %copy.9 = f32[1,64,1024]{2,1,0:T(8,128)} copy(f32[1,64,1024]{2,1,0:T(8,128)S(1)} %bitcast.1) | data formatting | bytes 524288

commit v3 on v2

--- a/solution.py
+++ b/solution.py
@@ -15,6 +15,7 @@
 COLS = 1024
 SUB = 8
 LANE = 128
+EDGE = 16
 HALO = 10
 HIGH = HALO + ROWS
 ALL = HALO + ROWS + HALO
@@ -47,7 +48,7 @@
 def kernel(
     control_hbm, gain_hbm, north_hbm, east_hbm, land_hbm, region_hbm, tiles_hbm,
     out_ref,
-    control, gain, north, east, land, region, tiles,
+    control, gain, north, east, land, own_region, region, tiles,
     base, ua, ub, ca, cn, cs, ce, cw,
     low_past, high_past, carried, sent, got, gathered, column, mixed, returned,
     product, weights,
@@ -73,7 +74,7 @@
         pltpu.make_async_copy(east_hbm.at[0], east, in_sem.at[2]),
         pltpu.make_async_copy(gain_hbm.at[0], gain, in_sem.at[3]),
         pltpu.make_async_copy(control_hbm.at[0], control, in_sem.at[4]),
-        pltpu.make_async_copy(region_hbm, region.at[which], in_sem.at[5]),
+        pltpu.make_async_copy(region_hbm, own_region, in_sem.at[5]),
         pltpu.make_async_copy(tiles_hbm.at[:, which], tiles, in_sem.at[6]),
     ]
     for load in loads:
@@ -108,6 +109,13 @@
 
     partner = lax.rem(lev + LEVELS, FIELDS * LEVELS)
     pl.semaphore_signal(barrier, inc=1, device_id={"lev": partner}, device_id_type=MESH)
+    middle = jnp.logical_and(lev >= EDGE, lev < ROWS - EDGE)
+
+    @pl.when(middle)
+    def _():
+        other = lev + EDGE - 2 * EDGE * which
+        pl.semaphore_signal(barrier, inc=1, device_id={"lev": other}, device_id_type=MESH)
+
 
     def greet(shift, carry):
         pl.semaphore_signal(barrier, inc=1, device_id={"lev": group_peer(shift)}, device_id_type=MESH)
@@ -138,7 +146,7 @@
     def as_count(flag):
         return flag.astype(jnp.int32)
 
-    greeted = LEVELS + as_count(tile > 0) + as_count(tile < last)
+    greeted = LEVELS + as_count(middle) + as_count(tile > 0) + as_count(tile < last)
     greeted = greeted + 2 * (WIDE - 1) * (as_count(upper_end) + as_count(lower_end))
     greeted = greeted + 2 * (as_count(up_carrier) + as_count(down_carrier))
     pl.semaphore_wait(barrier, greeted)
@@ -181,9 +189,10 @@
     for a in range(WIDE - 1):
         pl.when(lower_end)(send_rim(a, 0, 1 + a, carried.at[0]).start)
         pl.when(upper_end)(send_rim(a, 1, -1 - a, carried.at[1]).start)
+    start_both(straight[3])
+    for a in range(WIDE - 1):
         pl.when(jnp.logical_and(has_lower, jnp.logical_not(lower_end)))(straight[a][0].start)
         pl.when(jnp.logical_and(has_upper, jnp.logical_not(upper_end)))(straight[a][1].start)
-    start_both(straight[3])
 
     def carry_on():
         for side, carrier in enumerate((down_carrier, up_carrier)):
@@ -193,12 +202,25 @@
                 pltpu.make_async_copy(carried.at[side], carried.at[side], carry_recv.at[side]).wait()
                 copy.start()
 
-    region_copy = pltpu.make_async_remote_copy(
-        src_ref=region.at[which], dst_ref=region.at[which],
-        send_sem=region_sem.at[0], recv_sem=region_sem.at[1],
-        device_id={"lev": partner}, device_id_type=MESH,
-    )
-    region_copy.start()
+    def send_region(slot, to, send):
+        return pltpu.make_async_remote_copy(
+            src_ref=own_region, dst_ref=region.at[slot],
+            send_sem=region_sem.at[send], recv_sem=region_sem.at[2 + slot],
+            device_id={"lev": to}, device_id_type=MESH,
+        )
+
+    outer_region = send_region(0, partner, 0)
+    inner_regions = send_region(1, lev - EDGE, 0), send_region(1, lev + EDGE, 1)
+
+    @pl.when(middle)
+    def _():
+        for copy in inner_regions:
+            copy.start()
+
+    @pl.when(jnp.logical_not(middle))
+    def _():
+        outer_region.start()
+        region[0] = own_region[...]
 
     @pl.when(tile == 0)
     def _():
@@ -211,36 +233,6 @@
         for a in range(4):
             base[a, SUB * HIGH :, :] = jnp.zeros((SUB * HALO, LANE), F32)
         got[1] = jnp.zeros(got.shape[1:], F32)
-
-    loads[6].wait()
-
-    def square(r, carry):
-        t = tiles[r]
-        m = lax.dot_general(
-            t, t, (((0,), (0,)), ((), ())), precision=lax.Precision.HIGHEST, preferred_element_type=F32
-        )
-        product[pl.ds(pl.multiple_of(r * LEVELS, LEVELS), LEVELS), :] = m
-        return carry
-
-    lax.fori_loop(0, REGIONS, square, 0)
-
-    def thirds(x):
-        one = x.astype(BF16)
-        rest = x - one.astype(F32)
-        two = rest.astype(BF16)
-        three = (rest - two.astype(F32)).astype(BF16)
-        return one, two, three
-
-    k_of = lax.broadcasted_iota(jnp.int32, (LEVELS, 6 * LEVELS), 0)
-    j_of = lax.broadcasted_iota(jnp.int32, (LEVELS, 6 * LEVELS), 1)
-    total = None
-    for part, groups in zip(thirds(product[...]), ((0, 1, 3), (2, 4), (5,))):
-        pick = jnp.zeros((LEVELS, 6 * LEVELS), F32)
-        for g in groups:
-            pick = pick + jnp.where(j_of == k_of + g * LEVELS, 1.0, 0.0)
-        spread = jnp.dot(part, pick.astype(BF16), preferred_element_type=F32)
-        total = spread if total is None else total + spread
-    weights[...] = total.astype(BF16)
 
     first_lane = (1, SUB, LANE)
     lane1 = lax.broadcasted_iota(jnp.int32, first_lane, 2)
@@ -311,17 +303,6 @@
         put_rows(ua, HALO, low)
         put_rows(ua, HIGH - HALO, high)
 
-    carry_on()
-    inner()
-    for pair in straight:
-        wait_both_recv(pair)
-    coefs(1, HALO + 1)
-    coefs(HIGH, ALL - 1)
-    outer(rows_of(base.at[3], 0, HALO), rows_of(base.at[3], HIGH, HALO))
-
-    for h in range(2):
-        gathered[h] = rows_of(ua, HALO + h * LEVELS, LEVELS)
-
     def regroup(src, dst, h, sems):
         def one(shift, carry):
             peer = lax.rem(mine + shift, LEVELS)
@@ -337,10 +318,6 @@
 
     def wait_half(ref, h, sem):
         pltpu.make_async_copy(ref.at[h], ref.at[h], sem).wait()
-
-    for h in range(2):
-        regroup(gathered, column, h, all_sem.at[0])
-    region_copy.wait()
 
     wide = 2 * LANE
     column2 = column.reshape(2 * LEVELS * SUB, LANE)
@@ -365,17 +342,66 @@
             mixed2[pl.ds(start + q, LEVELS, stride=SUB), :] = y[:, q * LANE : (q + 1) * LANE]
         return carry
 
-    for h in range(2):
+    def blend(h):
         wait_half(column, h, all_sem.at[0, 1, h])
         lax.fori_loop(h * SUB // 2, (h + 1) * SUB // 2, mix, 0)
-        regroup(mixed, returned, h, all_sem.at[1])
-    for h in range(2):
-        wait_half(returned, h, all_sem.at[1, 1, h])
-
-    for h in range(2):
-        o = rows_of(base.at[2], HALO + h * LEVELS, LEVELS)
-        put_rows(ua, HALO + h * LEVELS, o * returned[h])
-
+
+    carry_on()
+    inner()
+    gathered[1] = rows_of(ua, HALO + EDGE, LEVELS)
+    regroup(gathered, column, 1, all_sem.at[0])
+
+    loads[6].wait()
+
+    def square(r, carry):
+        t = tiles[r]
+        m = lax.dot_general(
+            t, t, (((0,), (0,)), ((), ())), precision=lax.Precision.HIGHEST, preferred_element_type=F32
+        )
+        product[pl.ds(pl.multiple_of(r * LEVELS, LEVELS), LEVELS), :] = m
+        return carry
+
+    lax.fori_loop(0, REGIONS, square, 0, unroll=True)
+
+    def thirds(x):
+        one = x.astype(BF16)
+        rest = x - one.astype(F32)
+        two = rest.astype(BF16)
+        three = (rest - two.astype(F32)).astype(BF16)
+        return one, two, three
+
+    k_of = lax.broadcasted_iota(jnp.int32, (LEVELS, 6 * LEVELS), 0)
+    j_of = lax.broadcasted_iota(jnp.int32, (LEVELS, 6 * LEVELS), 1)
+    total = None
+    for part, groups in zip(thirds(product[...]), ((0, 1, 3), (2, 4), (5,))):
+        pick = jnp.zeros((LEVELS, 6 * LEVELS), F32)
+        for g in groups:
+            pick = pick + jnp.where(j_of == k_of + g * LEVELS, 1.0, 0.0)
+        spread = jnp.dot(part, pick.astype(BF16), preferred_element_type=F32)
+        total = spread if total is None else total + spread
+    weights[...] = total.astype(BF16)
+    for pair in straight:
+        wait_both_recv(pair)
+    coefs(1, HALO + 1)
+    coefs(HIGH, ALL - 1)
+    outer(rows_of(base.at[3], 0, HALO), rows_of(base.at[3], HIGH, HALO))
+    gathered[0, :EDGE] = rows_of(ua, HALO, EDGE)
+    gathered[0, EDGE:] = rows_of(ua, HIGH - EDGE, EDGE)
+    regroup(gathered, column, 0, all_sem.at[0])
+    inner_regions[0].wait_recv()
+    blend(1)
+    pl.when(middle)(outer_region.wait_recv)
+    blend(0)
+    regroup(mixed, returned, 0, all_sem.at[1])
+    regroup(mixed, returned, 1, all_sem.at[1])
+
+    def take(h, first, start, count):
+        o = rows_of(base.at[2], HALO + start, count)
+        put_rows(ua, HALO + start, o * returned[h, first : first + count])
+
+    wait_half(returned, 0, all_sem.at[1, 1, 0])
+    take(0, 0, 0, EDGE)
+    take(0, EDGE, ROWS - EDGE, EDGE)
     sent[0] = ua[SUB * HALO : 2 * SUB * HALO, :]
     sent[1] = ua[SUB * (HIGH - HALO) : SUB * HIGH, :]
     swap = tuple(
@@ -387,6 +413,8 @@
         for side in range(2)
     )
     start_both(swap)
+    wait_half(returned, 1, all_sem.at[1, 1, 1])
+    take(1, 0, EDGE, LEVELS)
     inner()
     wait_both_recv(swap)
     outer(got[0].reshape(HALO, SUB, LANE), got[1].reshape(HALO, SUB, LANE))
@@ -407,6 +435,8 @@
     for pair in straight:
         wait_both_send(pair)
     wait_both_send(swap)
+    inner_regions[0].wait_send()
+    pl.when(middle)(inner_regions[1].wait_send)
     for side, carrier in enumerate((down_carrier, up_carrier)):
         pl.when(carrier)(forward(side).wait_send)
 
@@ -424,6 +454,7 @@
         scratch_shapes=[
             raw, raw, raw, raw,
             pltpu.VMEM((ROWS, COLS), jnp.int32),
+            pltpu.VMEM((1, COLS), jnp.int32),
             pltpu.VMEM((2, 1, COLS), jnp.int32),
             pltpu.VMEM((REGIONS, LEVELS, LEVELS), F32),
             pltpu.VMEM((4, ALL * SUB, LANE), F32),
@@ -441,7 +472,7 @@
             pltpu.SemaphoreType.DMA((2,)),
             pltpu.SemaphoreType.DMA((2,)),
             pltpu.SemaphoreType.DMA((2,)),
-            pltpu.SemaphoreType.DMA((2,)),
+            pltpu.SemaphoreType.DMA((4,)),
             pltpu.SemaphoreType.DMA((2, 2, 2)),
         ],
         compiler_params=pltpu.CompilerParams(

time: 50.7 us -> 48.8 us (0.963)
  Pallas kernels: 49.7 us -> 47.7 us
    pallas_call x1, Pallas kernels: 49.7 us -> 47.7 us  [body(): pl.pallas_call(kernel, out_shape=jax.ShapeDtypeStruct((ROWS, COLS), F32),...]
where the time goes in v3:
time: 48.8 us; the launch traced here: 48.4 us
  Pallas kernels  47.7 us (98%)
  local copies, waits for them, and re-layouts  0.71 us (1%)
    pallas_call x1, Pallas kernels, body(): pl.pallas_call(kernel, out_shape=jax.ShapeDtypeStruct((ROWS, COLS), F32),...  47.7 us

profile of v3, /device:TPU:6, one launch (start us, length us, event | category | flops | bytes accessed | tf_op | source)
XLA Modules:
  0.0 48.4 jit_solution(12494377109412620419)
XLA Ops:
  0.0 47.7 %covariance.1 = f32[64,1024]{1,0:T(8,128)S(1)} custom-call(f32[1,64,1024]{2,1,0:T(8,128)} %control_hbm.1, f32[1,64,1024]{2,1,0:T(8,128)} %gain_hbm.1, f32[1,64,1024]{2,1,0:T(8,128)} %north_hbm.1, f32[1,64,1024]{2,1,0:T(8,128)} %east_hbm.1, s32[1,64,1024]{2,1,0:T(8,128)} %land_hbm.1, s32[1,1024]{1,0:T(1,128)} %region_hbm.1, f32[16,2,32,32]{3,2,1,0:T(8,128)} %tiles_hbm.1), custom_call_target="tpu_custom_call" | custom-call | tf_op jit(solution)/shard_map/covariance/pallas_call | solution.py:449
  47.7 0.7 %copy.9 = f32[1,64,1024]{2,1,0:T(8,128)} copy(f32[1,64,1024]{2,1,0:T(8,128)S(1)} %bitcast.1) | data formatting | bytes 524288

commit v4 on v3

--- a/solution.py
+++ b/solution.py
@@ -140,7 +140,7 @@
             ua[to, :] = start
         return carry
 
-    lax.fori_loop(0, ROWS // SUB, relayout, 0)
+    lax.fori_loop(0, ROWS // SUB, relayout, 0, unroll=True)
     loads[5].wait()
 
     def as_count(flag):
@@ -344,7 +344,7 @@
 
     def blend(h):
         wait_half(column, h, all_sem.at[0, 1, h])
-        lax.fori_loop(h * SUB // 2, (h + 1) * SUB // 2, mix, 0)
+        lax.fori_loop(h * SUB // 2, (h + 1) * SUB // 2, mix, 0, unroll=True)
 
     carry_on()
     inner()
@@ -426,7 +426,7 @@
             out_ref[at] = gain[at] * ua[pl.ds((HALO + r) * SUB + c, SUB, stride=SUB), :]
         return carry
 
-    lax.fori_loop(0, ROWS // SUB, finish, 0)
+    lax.fori_loop(0, ROWS // SUB, finish, 0, unroll=True)
 
     for ref, sems in ((gathered, all_sem.at[0]), (mixed, all_sem.at[1])):
         for h in range(2):

time: 48.8 us -> 48.2 us (0.988)
  Pallas kernels: 47.7 us -> 47.2 us
    pallas_call x1, Pallas kernels: 47.7 us -> 47.2 us  [body(): pl.pallas_call(kernel, out_shape=jax.ShapeDtypeStruct((ROWS, COLS), F32),...]
where the time goes in v4:
time: 48.2 us; the launch traced here: 47.9 us
  Pallas kernels  47.2 us (98%)
  local copies, waits for them, and re-layouts  0.71 us (1%)
    pallas_call x1, Pallas kernels, body(): pl.pallas_call(kernel, out_shape=jax.ShapeDtypeStruct((ROWS, COLS), F32),...  47.2 us

profile of v4, /device:TPU:6, one launch (start us, length us, event | category | flops | bytes accessed | tf_op | source)
XLA Modules:
  0.0 47.9 jit_solution(7311661979358064215)
XLA Ops:
  0.0 47.2 %covariance.1 = f32[64,1024]{1,0:T(8,128)S(1)} custom-call(f32[1,64,1024]{2,1,0:T(8,128)} %control_hbm.1, f32[1,64,1024]{2,1,0:T(8,128)} %gain_hbm.1, f32[1,64,1024]{2,1,0:T(8,128)} %north_hbm.1, f32[1,64,1024]{2,1,0:T(8,128)} %east_hbm.1, s32[1,64,1024]{2,1,0:T(8,128)} %land_hbm.1, s32[1,1024]{1,0:T(1,128)} %region_hbm.1, f32[16,2,32,32]{3,2,1,0:T(8,128)} %tiles_hbm.1), custom_call_target="tpu_custom_call" | custom-call | tf_op jit(solution)/shard_map/covariance/pallas_call | solution.py:449
  47.2 0.7 %copy.9 = f32[1,64,1024]{2,1,0:T(8,128)} copy(f32[1,64,1024]{2,1,0:T(8,128)S(1)} %bitcast.1) | data formatting | bytes 524288

commit v5 on v4

--- a/solution.py
+++ b/solution.py
@@ -304,17 +304,22 @@
         put_rows(ua, HIGH - HALO, high)
 
     def regroup(src, dst, h, sems):
-        def one(shift, carry):
+        def send(shift):
             peer = lax.rem(mine + shift, LEVELS)
             pltpu.make_async_remote_copy(
                 src_ref=src.at[h, peer], dst_ref=dst.at[h, mine],
                 send_sem=sems.at[0, h], recv_sem=sems.at[1, h],
                 device_id={"lev": which * LEVELS + peer}, device_id_type=MESH,
             ).start()
+
+        def six(i, carry):
+            for j in range(6):
+                send(1 + 6 * i + j)
             return carry
 
         pltpu.make_async_copy(src.at[h, mine], dst.at[h, mine], sems.at[1, h]).start()
-        lax.fori_loop(1, LEVELS, one, 0)
+        lax.fori_loop(0, (LEVELS - 1) // 6, six, 0)
+        send(LEVELS - 1)
 
     def wait_half(ref, h, sem):
         pltpu.make_async_copy(ref.at[h], ref.at[h], sem).wait()

time: 48.2 us -> 48.2 us (level)
  no operation moved by 1% of the time
where the time goes in v5:
time: 48.2 us; the launch traced here: 47.7 us
  Pallas kernels  47 us (98%)
  local copies, waits for them, and re-layouts  0.71 us (1%)
    pallas_call x1, Pallas kernels, body(): pl.pallas_call(kernel, out_shape=jax.ShapeDtypeStruct((ROWS, COLS), F32),...  47 us

profile of v5, /device:TPU:6, one launch (start us, length us, event | category | flops | bytes accessed | tf_op | source)
XLA Modules:
  0.0 47.7 jit_solution(521981795360677892)
XLA Ops:
  0.0 47.0 %covariance.1 = f32[64,1024]{1,0:T(8,128)S(1)} custom-call(f32[1,64,1024]{2,1,0:T(8,128)} %control_hbm.1, f32[1,64,1024]{2,1,0:T(8,128)} %gain_hbm.1, f32[1,64,1024]{2,1,0:T(8,128)} %north_hbm.1, f32[1,64,1024]{2,1,0:T(8,128)} %east_hbm.1, s32[1,64,1024]{2,1,0:T(8,128)} %land_hbm.1, s32[1,1024]{1,0:T(1,128)} %region_hbm.1, f32[16,2,32,32]{3,2,1,0:T(8,128)} %tiles_hbm.1), custom_call_target="tpu_custom_call" | custom-call | tf_op jit(solution)/shard_map/covariance/pallas_call | solution.py:454
  47.0 0.7 %copy.9 = f32[1,64,1024]{2,1,0:T(8,128)} copy(f32[1,64,1024]{2,1,0:T(8,128)S(1)} %bitcast.1) | data formatting | bytes 524288
